TPU v7x, 32 devices: a whole 2x2x4 slice. The times are simulated.
32 devices in a mesh: groups: 2 (over x), gy: 16 (over z, y, core).
Axes of the slice: x: 2, y: 2, z: 4, core: 2. Of those that a mesh axis runs over, the one named last changes fastest.
Arguments:
- tiles: bfloat16 [1024, 16, 128], P(('groups', 'gy')), parts along dimension 0, may hold values from -6 to 6
- entry_dest: int32 [1024, 1], P('groups'), parts along dimension 0, may hold values from 0 to 15; in each aligned block of 32 rows (0 to 31, 32 to 63, ...) at most 4 rows name the same one
- entry_tile: int32 [1024], P('groups'), parts along dimension 0, may hold values from 0 to 31
- entry_z: int32 [1024], P('groups'), parts along dimension 0, may hold values from 0 to 3
- entry_xb: int32 [1024], P('groups'), parts along dimension 0, may hold values from 0 to 3
- entry_ky: int32 [1024], P('groups'), parts along dimension 0, may hold values from 0 to 7
- entry_kx: int32 [1024], P('groups'), parts along dimension 0, may hold values from 0 to 7
- wy_table: bfloat16 [8, 8, 16], replicated, may hold values from 0 to 1
- wx_table: bfloat16 [8, 128, 128], replicated, may hold values from 0 to 1
- w_first: bfloat16 [32, 1, 3, 3, 3], replicated, may hold values from -1.25 to 1.25
- b_first: float32 [32], replicated, may hold values from -1.5 to 1.5
- w_second: bfloat16 [32, 32, 3, 3, 3], replicated, may hold values from -0.21875 to 0.21875
- b_second: float32 [32], replicated, may hold values from -1.5 to 1.5
- w_third: bfloat16 [32, 32, 3, 3, 3], replicated, may hold values from -0.21875 to 0.21875
- b_third: float32 [32], replicated, may hold values from -1.5 to 1.5
Outputs:
- affinity_features: bfloat16 [32, 8, 128, 512], P(None, 'groups', 'gy'), parts along dimension 1
There are 2 independent parts, one for each index of `groups`. A program takes and returns all parts, laid end to end along the dimension named above; an argument that names none is the same for every part. Nothing has to cross between parts.
Inputs may be any that keep to these rules, and one draw needn't show every extreme that they name: `entry_dest`: rows 32 * s to 32 * s + 31 are the entries of the tiles of device s of gy; among one device's rows no brick is named more than 4 times, a bound that some block reaches.
All inputs are finite; a program needn't handle non-finite values.
Results may differ from a plain program's by a relative error of at most 0.0064.
Values may be sent and summed in bfloat16 or wider, within the bound.
A program may use at most 64 MiB of HBM per device.

v0:
```python
import jax
import jax.numpy as jnp
from jax import lax
from jax.sharding import PartitionSpec as P

X = 512
YB = 8
Z = 4
CAP = 4


def with_halo(cells, sides, width):
    for axis, dim in sides:
        count = lax.axis_size(axis)
        ends = count - 1
        head = lax.slice_in_dim(cells, 0, width, axis=dim)
        tail = lax.slice_in_dim(cells, cells.shape[dim] - width, cells.shape[dim], axis=dim)
        cells = jnp.concatenate(
            [
                lax.ppermute(tail, axis, [(i, (i + 1) % count) for i in range(ends)]),
                cells,
                lax.ppermute(head, axis, [((i + 1) % count, i) for i in range(ends)]),
            ],
            axis=dim,
        )
    return cells


def convolve(padded, weight, bias):
    result = lax.conv_general_dilated(
        padded[None],
        weight,
        (1, 1, 1),
        ((1, 1), (0, 0), (1, 1)),
        dimension_numbers=("NCDHW", "OIDHW", "NCDHW"),
        preferred_element_type=jnp.float32,
    )[0]
    return jax.nn.relu(result + bias[:, None, None, None])


def on_device(
    tiles,
    entry_dest,
    entry_tile,
    entry_z,
    entry_xb,
    entry_ky,
    entry_kx,
    wy_table,
    wx_table,
    w_first,
    b_first,
    w_second,
    b_second,
    w_third,
    b_third,
):
    devices_gy = lax.axis_size("gy")
    own_index = lax.axis_index("gy")
    tiles_dev, tile_rows, tile_cols = tiles.shape
    per_device = entry_dest.shape[0] // devices_gy
    slot_total = devices_gy * CAP
    target_brick = entry_dest[:, 0].reshape(devices_gy, per_device)
    later_pos = lax.broadcasted_iota(jnp.int32, (per_device, per_device), 0)
    earlier_pos = lax.broadcasted_iota(jnp.int32, (per_device, per_device), 1)
    same_brick = (target_brick[:, :, None] == target_brick[:, None, :]) & (earlier_pos < later_pos)[
        None
    ]
    slot_rank = jnp.sum(same_brick, axis=2, dtype=jnp.int32)
    capacity_iota = lax.broadcasted_iota(jnp.int32, (1, CAP, 1), 1)
    matched = (
        (target_brick == own_index)[:, None, :] & (slot_rank[:, None, :] == capacity_iota)
    ).astype(jnp.float32)
    slot_live = jnp.sum(matched, axis=2).reshape(-1) > 0.5

    def slot_field(field):
        return (
            jnp.sum(matched * field.reshape(devices_gy, 1, per_device).astype(jnp.float32), axis=2)
            .reshape(-1)
            .astype(jnp.int32)
        )

    slot_z = slot_field(entry_z)
    slot_xb = slot_field(entry_xb)
    slot_ky = slot_field(entry_ky)
    slot_kx = slot_field(entry_kx)
    local_tiles = tiles.reshape(tiles_dev, tile_rows * tile_cols)
    own_brick = lax.dynamic_index_in_dim(target_brick, own_index, 0, keepdims=False)
    own_rank = lax.dynamic_index_in_dim(slot_rank, own_index, 0, keepdims=False)
    own_tile = lax.dynamic_index_in_dim(
        entry_tile.reshape(devices_gy, per_device), own_index, 0, keepdims=False
    )
    slot_target = own_brick * CAP + own_rank
    chooser = (
        lax.broadcasted_iota(jnp.int32, (slot_total, per_device), 0) == slot_target[None, :]
    ).astype(jnp.bfloat16)
    tile_choice = (
        own_tile[:, None] == lax.broadcasted_iota(jnp.int32, (per_device, tiles_dev), 1)
    ).astype(jnp.bfloat16)
    pick_matrix = jnp.dot(chooser, tile_choice, preferred_element_type=jnp.float32).astype(
        jnp.bfloat16
    )
    send_buffer = jnp.dot(pick_matrix, local_tiles, preferred_element_type=jnp.float32).astype(
        jnp.bfloat16
    )
    send_buffer = send_buffer.reshape(devices_gy, CAP, tile_rows * tile_cols)
    arrived = lax.all_to_all(send_buffer, "gy", split_axis=0, concat_axis=0, tiled=True).reshape(
        slot_total, tile_rows, tile_cols
    )
    ky_onehot = (
        slot_ky[:, None] == lax.broadcasted_iota(jnp.int32, (1, wy_table.shape[0]), 1)
    ).astype(jnp.bfloat16)
    vertical = jnp.einsum(
        "mk,kys->mys", ky_onehot, wy_table, preferred_element_type=jnp.float32
    ).astype(jnp.bfloat16)
    row_samples = jnp.einsum(
        "mys,msw->myw", vertical, arrived, preferred_element_type=jnp.float32
    ).astype(jnp.bfloat16)
    kx_onehot = (
        slot_kx[:, None] == lax.broadcasted_iota(jnp.int32, (1, wx_table.shape[0]), 1)
    ).astype(jnp.bfloat16)
    horizontal = jnp.einsum(
        "mk,ksp->msp", kx_onehot, wx_table, preferred_element_type=jnp.float32
    ).astype(jnp.bfloat16)
    patches = jnp.einsum(
        "myw,mwp->myp", row_samples, horizontal, preferred_element_type=jnp.float32
    )
    x_blocks = X // tile_cols
    placement = (
        (slot_z * x_blocks + slot_xb)[:, None]
        == lax.broadcasted_iota(jnp.int32, (1, Z * x_blocks), 1)
    ) & slot_live[:, None]
    rendered = jnp.einsum(
        "mq,myp->qyp", placement.astype(jnp.float32), patches, precision=lax.Precision.HIGHEST
    )
    image = (
        rendered.reshape(Z, x_blocks, YB, tile_cols)
        .transpose(0, 2, 1, 3)
        .reshape(Z, YB, X)
        .astype(jnp.bfloat16)
    )
    extended = with_halo(image[None], (("gy", 2),), 3)
    features = extended
    for weight, bias, extra_rows in (
        (w_first, b_first, 2),
        (w_second, b_second, 1),
        (w_third, b_third, 0),
    ):
        result = convolve(features, weight, bias)
        row_count = result.shape[2]
        global_row = own_index * YB - extra_rows + lax.broadcasted_iota(jnp.int32, (row_count,), 0)
        inside = (global_row >= 0) & (global_row < YB * devices_gy)
        features = jnp.where(inside[None, None, :, None], result, jnp.zeros_like(result)).astype(
            jnp.bfloat16
        )
    return features


def solution(mesh):
    return jax.shard_map(
        on_device,
        mesh=mesh,
        in_specs=(
            P(("groups", "gy"), None, None),
            P("groups", None),
            P("groups"),
            P("groups"),
            P("groups"),
            P("groups"),
            P("groups"),
            P(),
            P(),
            P(),
            P(),
            P(),
            P(),
            P(),
            P(),
        ),
        out_specs=P(None, "groups", "gy", None),
        check_vma=False,
    )
```

profile of v0, /device:TPU:13, one launch (start us, length us, event | category | flops | bytes accessed | tf_op | source)
XLA Modules:
  0.0 104.1 jit_solution(4561536459919610972)
XLA Ops:
  0.0 0.0 copy-start
  0.0 0.0 copy-start.8
  0.0 0.0 copy-start.6
  0.0 0.0 copy-start.5
  0.0 0.5 broadcast.173
  0.6 1.3 %reduce.3 = s32[512]{0:T(512)S(1)} reduce(s32[512,1]{0,1:T(1,128)} %param.16, s32[]{:T(128)} %broadcast.173), dimensions={1}, to_apply=%param.16.reduce_sub_computation.3 | reduce | bytes 4100 | tf_op args[1]
  1.9 0.1 reshape_squeeze.3
  2.0 0.8 reshape.144
  2.7 0.5 convert_reduce_fusion
  3.2 1.4 %convolution_convert_fusion = bf16[64,2048]{1,0:T(8,128)(2,1)S(1)} fusion(bf16[4,8,16,128]{3,2,1,0:T(8,128)(2,1)} %bitcast.62, s32[32]{0:T(128)S(1)} %get-tuple-element.17, s32[32]{0:T(128)S(1)} %get-tuple-element.16), kind=kOutput, calls=%fused_computation.33 | convolution fusion | flops 8655872 | bytes 393472 | tf_op jit(solution)/shard_map/dot_general | solution.py:103
  4.6 0.8 reshape.146
  5.4 6.5 %all-to-all-start = ((bf16[16,4,2048]{2,1,0:T(4,128)(2,1)}), bf16[16,4,2048]{2,1,0:T(4,128)(2,1)S(1)}, u32[]{:S(2)}, u32[]{:S(2)}) async-start(bf16[16,4,2048]{2,1,0:T(4,128)(2,1)} %reshape.146), calls=%async_computation | async-start | bytes 524288 | tf_op jit(solution)/shard_map/all_to_all | solution.py:107
  12.0 0.7 convert_element_type.137
  12.7 0.7 convert_element_type.140
  13.4 0.7 convert_element_type.144
  14.0 0.7 convert_element_type.152
  14.7 0.1 convert_element_type.153
  14.8 0.1 convert_element_type.145
  14.9 0.1 convert_element_type.141
  15.0 0.1 convert_element_type.138
  15.0 0.1 convert_reduce_fusion.1
  15.2 0.1 copy.41
  15.3 0.1 gt.15
  15.4 0.1 copy.40
  15.5 0.1 add.85
  15.6 0.1 copy.42
  15.7 0.1 convert_element_type.147
  15.8 0.1 copy.45
  15.8 0.1 convert_element_type.155
  15.9 0.9 convolution_convert_fusion.3
  16.9 0.1 copy.44
  17.0 0.5 compare_and_fusion.2
  17.6 0.0 copy-done
  17.6 0.8 convolution_convert_fusion.1
  18.3 1.6 %all-to-all-done = bf16[16,4,2048]{2,1,0:T(4,128)(2,1)S(1)} async-done(((bf16[16,4,2048]{2,1,0:T(4,128)(2,1)}), bf16[16,4,2048]{2,1,0:T(4,128)(2,1)S(1)}, u32[]{:S(2)}, u32[]{:S(2)}) %all-to-all-start) | async-done | bytes 262176 | tf_op jit(solution)/shard_map/all_to_all | solution.py:107
  19.9 0.2 reshape.147
  20.1 1.9 %fusion.36 = f32[64,8,128]{2,1,0:T(8,128)S(1)} fusion(bf16[64,128,128]{2,0,1:T(8,128)(2,1)S(1)} %convolution_convert_fusion.1, bf16[64,8,16]{2,1,0:T(8,128)(2,1)S(1)} %copy.44, bf16[64,16,128]{2,1,0:T(8,128)(2,1)S(1)} %reshape.147), kind=kOutput, calls=%fused_computation.39 | convolution fusion | flops 18939904 | bytes 2637824 | tf_op jit(solution)/shard_map/myw,mwp->myp/dot_general | solution.py:125
  22.0 0.2 convolution_convert_fusion.4
  22.3 3.7 %collective-permute-start = (bf16[1,4,3,512]{3,1,2,0:T(4,128)(2,1)S(1)}, bf16[1,4,3,512]{3,1,2,0:T(4,128)(2,1)S(1)}, u32[]{:S(2)}, u32[]{:S(2)}) collective-permute-start(bf16[1,4,3,512]{3,1,2,0:T(4,128)(2,1)S(1)} %get-tuple-element.14), channel_id=1, source_target_pairs={{0,1},{1,2},{2,3},{3,4},{4,5},{5,6},{6,7},{7,8},{8,9},{9,10},{10,1... | collective-permute-start | bytes 36872 | tf_op jit(solution)/shard_map/ppermute | solution.py:20
  26.0 2.1 %collective-permute-start.1 = (bf16[1,4,3,512]{3,1,2,0:T(4,128)(2,1)S(1)}, bf16[1,4,3,512]{3,1,2,0:T(4,128)(2,1)S(1)}, u32[]{:S(2)}, u32[]{:S(2)}) collective-permute-start(bf16[1,4,3,512]{3,1,2,0:T(4,128)(2,1)S(1)} %get-tuple-element.15), channel_id=1, source_target_pairs={{1,0},{2,1},{3,2},{4,3},{5,4},{6,5},{7,6},{8,7},{9,8},{10,9},{11,1... | collective-permute-start | bytes 36872 | tf_op jit(solution)/shard_map/ppermute | solution.py:22
  28.1 0.0 collective-permute-done
  28.1 3.8 %collective-permute-done.1 = bf16[1,4,3,512]{3,1,2,0:T(4,128)(2,1)S(1)} collective-permute-done((bf16[1,4,3,512]{3,1,2,0:T(4,128)(2,1)S(1)}, bf16[1,4,3,512]{3,1,2,0:T(4,128)(2,1)S(1)}, u32[]{:S(2)}, u32[]{:S(2)}) %collective-permute-start.1) | collective-permute-done | bytes 12320 | tf_op jit(solution)/shard_map/ppermute | solution.py:22
  32.0 0.1 pad
  32.1 0.2 reshape.150
  32.3 0.1 fusion.44
  32.4 2.1 %copy.50 = bf16[1,4,14,8,67]{3,0,4,2,1:T(2,128)(2,1)S(1)} copy(bf16[1,4,14,8,67]{4,3,1,2,0:T(8,128)(2,1)S(1)} %fusion.44) | data formatting | bytes 120064 | tf_op jit(solution)/shard_map/conv_general_dilated | solution.py:30
  34.5 0.0 copy-done.8
  34.5 0.0 copy-done.6
  34.5 0.0 copy-done.5
  34.5 0.0 copy-start.3
  34.6 0.0 copy-start.7
  34.6 22.6 %select_bitcast_fusion = bf16[4,12,1,8,65,32]{5,3,4,1,0,2:T(8,128)(2,1)S(1)} fusion(f32[32]{0:T(128)S(1)} %copy-done.6, bf16[1,4,14,8,67]{3,0,4,2,1:T(2,128)(2,1)S(1)} %copy.50, pred[12]{0:T(512)(128)(4,1)S(1)} %compare_and_fusion, pred[8,65]{0,1:T(8,128)(4,1)S(1)} %copy-done.8, bf16[32,1,3,3,3]{0,4,3,2,1:T(4,128)(2,1)S(1)} %copy-done.5), kind=kOutput, calls=%fused_computation.19 | convolution fusion | flops 40734720 | bytes 1659860 | tf_op jit(solution)/shard_map/conv_general_dilated | solution.py:30
  57.2 0.0 copy-done.3
  57.2 0.0 copy-done.7
  57.2 0.0 copy-start.4
  57.2 18.6 %fusion.27 = bf16[4,10,1,8,65,32]{5,3,4,1,0,2:T(8,128)(2,1)S(1)} fusion(f32[32]{0:T(128)S(1)} %copy-done.7, pred[10]{0:T(512)(128)(4,1)S(1)} %compare_and_fusion.1, pred[8,65]{0,1:T(8,128)(4,1)S(1)} %copy-done.8, bf16[32,32,3,3,3]{1,0,4,3,2:T(8,128)(2,1)S(1)} %copy-done.3, bf16[4,12,1,7,1,32]{5,3,4,1,0,2:T(8,128)(2,1)S(1)} %get-tuple-element.11, ...), kind=kOutput, calls=%fused_computation.30 | convolution fusion | flops 970024960 | bytes 3027602 | tf_op jit(solution)/shard_map/conv_general_dilated | solution.py:30
  75.9 0.0 copy-done.4
  75.9 14.7 %fusion.17 = f32[4,8,8,65,32]{4,2,3,1,0:T(8,128)} fusion(bf16[32,32,3,3,3]{1,0,4,3,2:T(8,128)(2,1)S(1)} %copy-done.4, bf16[4,10,1,7,1,32]{5,3,4,1,0,2:T(8,128)(2,1)S(1)} %get-tuple-element.13, bf16[4,10,1,7,1,32]{5,3,4,1,0,2:T(8,128)(2,1)S(1)} %get-tuple-element.12, bf16[4,10,1,8,65,32]{5,3,4,1,0,2:T(8,128)(2,1)S(1)} %fusion.27), kind=kOutput, calls=%fused_computation.22 | convolution fusion | flops 773632000 | bytes 3552256 | tf_op jit(solution)/shard_map/conv_general_dilated | solution.py:30
  90.6 7.9 %copy.52 = f32[4,8,8,65,32]{3,2,4,1,0:T(8,128)} copy(f32[4,8,8,65,32]{4,2,3,1,0:T(8,128)} %fusion.17) | data formatting | bytes 4259840 | tf_op jit(solution)/shard_map/conv_general_dilated | solution.py:30
  98.5 3.6 %reshape.160 = f32[4,8,1,520,32]{3,4,1,0,2:T(8,128)S(1)} reshape(f32[4,8,8,65,32]{3,2,4,1,0:T(8,128)} %copy.52) | data formatting | bytes 4259840 | tf_op jit(solution)/shard_map/conv_general_dilated | solution.py:30
  102.2 0.0 copy-done.1
  102.2 0.0 copy-done.2
  102.2 0.3 fusion.35
  102.5 1.5 %copy.53 = bf16[32,4,8,512]{3,2,1,0:T(8,128)(2,1)} copy(bf16[32,4,8,512]{3,0,2,1:T(8,128)(2,1)S(1)} %fusion.35) | data formatting | bytes 2097152 | tf_op jit(solution)/shard_map/convert_element_type | solution.py:153
  (17 shorter events, 0.3 us)
Async XLA Ops:
  0.0 17.6 %copy-start = (bf16[8,128,128]{2,1,0:T(8,128)(2,1)S(1)}, bf16[8,128,128]{2,1,0:T(8,128)(2,1)}, u32[]{:S(2)}) copy-start(bf16[8,128,128]{2,1,0:T(8,128)(2,1)} %param.23) | copy-start | bytes 786436
  0.0 34.5 %copy-start.8 = (pred[8,65]{0,1:T(8,128)(4,1)S(1)}, pred[8,65]{0,1:T(8,128)(4,1)}, u32[]{:S(2)}) copy-start(pred[8,65]{0,1:T(8,128)(4,1)} %constant.60) | copy-start | bytes 1564
  0.0 34.5 %copy-start.6 = (f32[32]{0:T(128)S(1)}, f32[32]{0:T(128)}, u32[]{:S(2)}) copy-start(f32[32]{0:T(128)} %param.25) | copy-start | bytes 388
  0.0 34.5 %copy-start.5 = (bf16[32,1,3,3,3]{0,4,3,2,1:T(4,128)(2,1)S(1)}, bf16[32,1,3,3,3]{0,4,3,2,1:T(4,128)(2,1)}, u32[]{:S(2)}) copy-start(bf16[32,1,3,3,3]{0,4,3,2,1:T(4,128)(2,1)} %param.24) | copy-start | bytes 5188
  5.4 14.5 %all-to-all-start = ((bf16[16,4,2048]{2,1,0:T(4,128)(2,1)}), bf16[16,4,2048]{2,1,0:T(4,128)(2,1)S(1)}, u32[]{:S(2)}, u32[]{:S(2)}) async-start(bf16[16,4,2048]{2,1,0:T(4,128)(2,1)} %reshape.146), calls=%async_computation | async-start | bytes 524288 | tf_op jit(solution)/shard_map/all_to_all | solution.py:107
  22.3 5.8 %collective-permute-start = (bf16[1,4,3,512]{3,1,2,0:T(4,128)(2,1)S(1)}, bf16[1,4,3,512]{3,1,2,0:T(4,128)(2,1)S(1)}, u32[]{:S(2)}, u32[]{:S(2)}) collective-permute-start(bf16[1,4,3,512]{3,1,2,0:T(4,128)(2,1)S(1)} %get-tuple-element.14), channel_id=1, source_target_pairs={{0,1},{1,2},{2,3},{3,4},{4,5},{5,6},{6,7},{7,8},{8,9},{9,10},{10,1... | collective-permute-start | bytes 36872 | tf_op jit(solution)/shard_map/ppermute | solution.py:20
  26.0 5.9 %collective-permute-start.1 = (bf16[1,4,3,512]{3,1,2,0:T(4,128)(2,1)S(1)}, bf16[1,4,3,512]{3,1,2,0:T(4,128)(2,1)S(1)}, u32[]{:S(2)}, u32[]{:S(2)}) collective-permute-start(bf16[1,4,3,512]{3,1,2,0:T(4,128)(2,1)S(1)} %get-tuple-element.15), channel_id=1, source_target_pairs={{1,0},{2,1},{3,2},{4,3},{5,4},{6,5},{7,6},{8,7},{9,8},{10,9},{11,1... | collective-permute-start | bytes 36872 | tf_op jit(solution)/shard_map/ppermute | solution.py:22
  34.5 22.7 %copy-start.3 = (bf16[32,32,3,3,3]{1,0,4,3,2:T(8,128)(2,1)S(1)}, bf16[32,32,3,3,3]{1,0,4,3,2:T(8,128)(2,1)}, u32[]{:S(2)}) copy-start(bf16[32,32,3,3,3]{1,0,4,3,2:T(8,128)(2,1)} %param.26) | copy-start | bytes 165892
  34.6 22.7 %copy-start.7 = (f32[32]{0:T(128)S(1)}, f32[32]{0:T(128)}, u32[]{:S(2)}) copy-start(f32[32]{0:T(128)} %param.27) | copy-start | bytes 388
  57.2 18.7 %copy-start.4 = (bf16[32,32,3,3,3]{1,0,4,3,2:T(8,128)(2,1)S(1)}, bf16[32,32,3,3,3]{1,0,4,3,2:T(8,128)(2,1)}, u32[]{:S(2)}) copy-start(bf16[32,32,3,3,3]{1,0,4,3,2:T(8,128)(2,1)} %param.28) | copy-start | bytes 165892
  98.5 3.6 %copy-start.1 = (f32[32]{0:T(128)S(1)}, f32[32]{0:T(128)}, u32[]{:S(2)}) copy-start(f32[32]{0:T(128)} %param.29) | copy-start | bytes 388
  98.5 3.6 %copy-start.2 = (pred[8]{0:T(512)(128)(4,1)S(1)}, pred[8]{0:T(512)(128)(4,1)}, u32[]{:S(2)}) copy-start(pred[8]{0:T(512)(128)(4,1)} %compare_and_fusion.2) | copy-start | bytes 28
where the time goes:
time: 105 us; the launch traced here: 104 us
  matrix products  61.1 us (58%)
  local copies, waits for them, and re-layouts  19.2 us (18%)
  starting transfers between devices  12.3 us (12%)
  other arithmetic  5.77 us (5%)
  waiting for transfers between devices  5.39 us (5%)
    conv_general_dilated x3, matrix products, convolve(): lax.conv_general_dilated(padded[None], weight, (1, 1, 1), ((1, 1), (0, 0)...  55.9 us
    conv_general_dilated x5, local copies, waits for them, and re-layouts, convolve(): lax.conv_general_dilated(padded[None], weight, (1, 1, 1), ((1, 1), (0, 0)...  13.9 us
    all_to_all x1, starting transfers between devices, on_device(): lax.all_to_all(send_buffer, 'gy', split_axis=0, concat_axis=0, tiled=True)  6.52 us
    ppermute x1, waiting for transfers between devices, with_halo(): lax.ppermute(head, axis, [((i + 1) % count, i) for i in range(ends)])  3.78 us
    ppermute x1, starting transfers between devices, with_halo(): lax.ppermute(tail, axis, [(i, (i + 1) % count) for i in range(ends)])  3.67 us
    convert_element_type x4, other arithmetic, slot_field(): field.reshape(devices_gy, 1, per_device).astype(jnp.float32)  2.74 us
    ppermute x1, starting transfers between devices, with_halo(): lax.ppermute(head, axis, [((i + 1) % count, i) for i in range(ends)])  2.1 us
  transfers between devices with their start and end apart: 3, of which 2 were waited for; matrix products, arithmetic and copies ran while one was open for 6% of the time, Pallas kernels for 0%

commit v1 on v0

--- a/solution.py
+++ b/solution.py
@@ -1,6 +1,9 @@
 import jax
 import jax.numpy as jnp
+import numpy as np
 from jax import lax
+from jax.experimental import pallas as pl
+from jax.experimental.pallas import tpu as pltpu
 from jax.sharding import PartitionSpec as P
 
 X = 512
@@ -26,16 +29,127 @@
     return cells
 
 
-def convolve(padded, weight, bias):
-    result = lax.conv_general_dilated(
-        padded[None],
-        weight,
-        (1, 1, 1),
-        ((1, 1), (0, 0), (1, 1)),
-        dimension_numbers=("NCDHW", "OIDHW", "NCDHW"),
+def first_taps():
+    taps = np.zeros((27, 2, Z, 3, 4, Z), np.float32)
+    for yo in range(2):
+        for zo in range(Z):
+            for c in range(3):
+                for b in range(3):
+                    for a in range(3):
+                        zi = zo + a - 1
+                        if 0 <= zi < Z:
+                            taps[(a * 3 + b) * 3 + c, yo, zo, c, yo + b, zi] = 1.0
+    return taps.reshape(27, 2 * Z, 12 * Z)
+
+
+def shifted(value):
+    lane = lax.broadcasted_iota(jnp.int32, value.shape, 1)
+    width = value.shape[1]
+    before = jnp.where(lane == 0, 0.0, pltpu.roll(value, 1, 1))
+    after = jnp.where(lane == width - 1, 0.0, pltpu.roll(value, width - 1, 1))
+    return before, value, after
+
+
+def convolutions(image_ref, taps_ref, band_ref, bias_ref, out_ref, band, first, second, third):
+    own_index = lax.axis_index("gy")
+    last_index = lax.axis_size("gy") - 1
+    channels = out_ref.shape[0]
+    plane = Z * channels
+    lane = lax.broadcasted_iota(jnp.int32, (band_ref.shape[1], plane), 1)
+    band[...] = jnp.zeros_like(band)
+    for layer in range(2):
+        source = band_ref[layer].astype(jnp.float32)
+        for zo in range(Z):
+            offset = (zo - 1) * channels
+            placed = source if offset == 0 else pltpu.roll(source, offset % plane, 1)
+            placed = jnp.where((lane >= offset) & (lane < offset + 3 * channels), placed, 0.0)
+            placed = placed.astype(jnp.bfloat16)
+            for c in range(3):
+                for b in range(3):
+                    block = placed[(c * 3 + b) * channels : (c * 3 + b + 1) * channels]
+                    for yo in range(2):
+                        rows = (yo * Z + zo) * channels
+                        cols = ((yo + b) * 3 + c) * plane
+                        band[layer, rows : rows + channels, cols : cols + plane] = block
+
+    def keep(result, target, pair, pairs, extra_rows):
+        result = jnp.maximum(result, 0.0)
+        for yo in range(2):
+            row = 2 * pair + yo - extra_rows
+            part = result[yo * plane : (yo + 1) * plane]
+            if row < 0:
+                part = jnp.where(own_index > 0, part, 0.0)
+            if row >= YB:
+                part = jnp.where(own_index < last_index, part, 0.0)
+            for c, moved in enumerate(shifted(part)):
+                start = ((2 * pair + yo) * 3 + c) * plane
+                target[start : start + plane, :] = moved.astype(jnp.bfloat16)
+
+    pieces = shifted(image_ref[...].astype(jnp.float32))
+    pairs = YB // 2 + 2
+    for pair in range(pairs):
+        window = jnp.concatenate(
+            [
+                piece[2 * pair * Z : (2 * pair + 4) * Z].astype(jnp.bfloat16)
+                for piece in pieces
+            ],
+            axis=0,
+        )
+        result = jnp.dot(taps_ref[...], window, preferred_element_type=jnp.float32)
+        keep(result + bias_ref[:, 0:1], first, pair, pairs, 2)
+    depth = 12 * plane
+    for pair in range(YB // 2 + 1):
+        window = first[6 * pair * plane : 6 * pair * plane + depth, :]
+        result = jnp.dot(band[0], window, preferred_element_type=jnp.float32)
+        keep(result + bias_ref[:, 1:2], second, pair, YB // 2 + 1, 1)
+    for pair in range(YB // 2):
+        window = second[6 * pair * plane : 6 * pair * plane + depth, :]
+        result = jnp.dot(band[1], window, preferred_element_type=jnp.float32)
+        result = jnp.maximum(result + bias_ref[:, 2:3], 0.0)
+        for yo in range(2):
+            for zo in range(Z):
+                rows = (yo * Z + zo) * channels
+                start = zo * YB + 2 * pair + yo
+                for block in range(third.shape[0]):
+                    third[block, pl.ds(start, channels, stride=Z * YB), :] = result[
+                        rows : rows + channels, block * 128 : (block + 1) * 128
+                    ]
+    for block in range(third.shape[0]):
+        out_ref[:, :, :, block * 128 : (block + 1) * 128] = (
+            third[block].reshape(channels, Z, YB, 128).astype(jnp.bfloat16)
+        )
+
+
+def network(image, w_first, b_first, w_second, b_second, w_third, b_third):
+    channels = w_first.shape[0]
+    width = image.shape[1]
+    plane = Z * channels
+    taps = jnp.einsum(
+        "ot,trk->rok",
+        w_first.reshape(channels, 27),
+        first_taps().astype(jnp.bfloat16),
         preferred_element_type=jnp.float32,
-    )[0]
-    return jax.nn.relu(result + bias[:, None, None, None])
+    )
+    taps = taps.astype(jnp.bfloat16).reshape(2 * plane, 12 * Z)
+    weights = jnp.stack([w_second, w_third]).transpose(0, 5, 4, 1, 3, 2)
+    weights = jnp.pad(weights, ((0, 0), (0, 0), (0, 0), (0, 0), (0, 1), (0, 0)))
+    weights = weights.reshape(2, 9 * channels, 4 * channels)
+    biases = jnp.tile(jnp.stack([b_first, b_second, b_third], axis=1), (2 * Z, 1))
+    vmem = pl.BlockSpec(memory_space=pltpu.VMEM)
+    return pl.pallas_call(
+        convolutions,
+        out_shape=jax.ShapeDtypeStruct((channels, Z, YB, width), jnp.bfloat16),
+        in_specs=[vmem] * 4,
+        out_specs=vmem,
+        scratch_shapes=[
+            pltpu.VMEM((2, 2 * plane, 12 * plane), jnp.bfloat16),
+            pltpu.VMEM((3 * plane * (YB + 4), width), jnp.bfloat16),
+            pltpu.VMEM((3 * plane * (YB + 2), width), jnp.bfloat16),
+            pltpu.VMEM((width // 128, plane * YB, 128), jnp.float32),
+        ],
+        compiler_params=pltpu.CompilerParams(vmem_limit_bytes=48 << 20),
+        name="network",
+    )(image, taps, weights, biases)
 
 
 def on_device(
@@ -140,20 +254,8 @@
         .astype(jnp.bfloat16)
     )
     extended = with_halo(image[None], (("gy", 2),), 3)
-    features = extended
-    for weight, bias, extra_rows in (
-        (w_first, b_first, 2),
-        (w_second, b_second, 1),
-        (w_third, b_third, 0),
-    ):
-        result = convolve(features, weight, bias)
-        row_count = result.shape[2]
-        global_row = own_index * YB - extra_rows + lax.broadcasted_iota(jnp.int32, (row_count,), 0)
-        inside = (global_row >= 0) & (global_row < YB * devices_gy)
-        features = jnp.where(inside[None, None, :, None], result, jnp.zeros_like(result)).astype(
-            jnp.bfloat16
-        )
-    return features
+    rows = extended[0].transpose(1, 0, 2).reshape((YB + 6) * Z, X)
+    return network(rows, w_first, b_first, w_second, b_second, w_third, b_third)
 
 
 def solution(mesh):

time: 105 us -> 40.6 us (0.39)
  the two profiles are of different devices: /device:TPU:13 before, /device:TPU:15 now
where the time goes in v1:
time: 40.6 us; the launch traced here: 40 us
  starting transfers between devices  12.1 us (30%)
  Pallas kernels  7.99 us (20%)
  matrix products  5.46 us (13%)
  local copies, waits for them, and re-layouts  5.35 us (13%)
  other arithmetic  4.88 us (12%)
  waiting for transfers between devices  3.93 us (10%)
    pallas_call x1, Pallas kernels, network(): pl.pallas_call(convolutions, out_shape=jax.ShapeDtypeStruct((channels, Z,...  7.99 us
    all_to_all x1, starting transfers between devices, on_device(): lax.all_to_all(send_buffer, 'gy', split_axis=0, concat_axis=0, tiled=True)  6.52 us
    ppermute x1, starting transfers between devices, with_halo(): lax.ppermute(tail, axis, [(i, (i + 1) % count) for i in range(ends)])  3.66 us
    ppermute x1, waiting for transfers between devices, with_halo(): lax.ppermute(head, axis, [((i + 1) % count, i) for i in range(ends)])  2.86 us
    convert_element_type x4, other arithmetic, slot_field(): field.reshape(devices_gy, 1, per_device).astype(jnp.float32)  2.74 us
    dot_general x1, matrix products, on_device(): jnp.einsum('myw,mwp->myp', row_samples, horizontal, preferred_element_typ...  1.95 us
    ppermute x1, starting transfers between devices, with_halo(): lax.ppermute(head, axis, [((i + 1) % count, i) for i in range(ends)])  1.92 us
    dot_general x1, matrix products, on_device(): jnp.dot(pick_matrix, local_tiles, preferred_element_type=jnp.float32)  1.42 us
  transfers between devices with their start and end apart: 3, of which 2 were waited for; matrix products, arithmetic and copies ran while one was open for 20% of the time, Pallas kernels for 0%

profile of v1, /device:TPU:15, one launch (start us, length us, event | category | flops | bytes accessed | tf_op | source)
XLA Modules:
  0.0 40.0 jit_solution(1208019030968565652)
XLA Ops:
  0.0 0.0 copy-start
  0.0 0.0 copy-start.3
  0.0 0.0 copy-start.2
  0.0 0.0 copy-start.1
  0.0 0.5 %broadcast.37 = s32[]{:T(128)} broadcast(s32[]{:T(128)} %constant.24.clone.1), dimensions={} | broadcast | bytes 8 | tf_op args[1]
  0.6 1.3 %reduce.3 = s32[512]{0:T(512)S(1)} reduce(s32[512,1]{0,1:T(1,128)} %param.17, s32[]{:T(128)} %broadcast.37), dimensions={1}, to_apply=%param.17.reduce_sub_computation.3 | reduce | bytes 4100 | tf_op args[1]
  1.9 0.1 reshape_squeeze.3
  2.0 0.8 %reshape.136 = s32[16,32]{1,0:T(8,128)S(1)} reshape(s32[512]{0:T(512)} %param.18) | data formatting | bytes 4096 | tf_op jit(solution)/shard_map/reshape | solution.py:205
  2.7 0.5 %convert_reduce_fusion = s32[16,32]{1,0:T(8,128)S(1)} fusion(s32[16,32]{1,0:T(8,128)S(1)} %reshape_squeeze.3, pred[32,32]{1,0:T(8,128)(4,1)S(1)} %iota_compare_fusion.5), kind=kLoop, calls=%fused_computation.12 | loop fusion | flops 65024 | bytes 5120 | tf_op jit(solution)/shard_map/reduce_sum | solution.py:183
  3.2 1.4 %convolution_convert_fusion = bf16[64,2048]{1,0:T(8,128)(2,1)S(1)} fusion(bf16[4,8,16,128]{3,2,1,0:T(8,128)(2,1)} %bitcast.50, s32[32]{0:T(128)S(1)} %get-tuple-element.13, s32[32]{0:T(128)S(1)} %get-tuple-element.12), kind=kOutput, calls=%fused_computation | convolution fusion | flops 8655872 | bytes 393472 | tf_op jit(solution)/shard_map/dot_general | solution.py:217
  4.6 0.8 %reshape.138 = bf16[16,4,2048]{2,1,0:T(4,128)(2,1)} reshape(bf16[64,2048]{1,0:T(8,128)(2,1)S(1)} %convolution_convert_fusion) | data formatting | bytes 524288 | tf_op jit(solution)/shard_map/reshape | solution.py:220
  5.4 6.5 %all-to-all-start = ((bf16[16,4,2048]{2,1,0:T(4,128)(2,1)}), bf16[16,4,2048]{2,1,0:T(4,128)(2,1)S(1)}, u32[]{:S(2)}, u32[]{:S(2)}) async-start(bf16[16,4,2048]{2,1,0:T(4,128)(2,1)} %reshape.138), calls=%async_computation | async-start | bytes 524288 | tf_op jit(solution)/shard_map/all_to_all | solution.py:221
  12.0 0.7 %convert_element_type.134 = f32[512]{0:T(512)S(1)} convert(s32[512]{0:T(512)} %param.19) | non-fusion elementwise | flops 512 | bytes 4096 | tf_op jit(solution)/shard_map/convert_element_type | solution.py:192
  12.7 0.1 convert_element_type.135
  12.7 0.7 %convert_element_type.137 = f32[512]{0:T(512)S(1)} convert(s32[512]{0:T(512)} %param.20) | non-fusion elementwise | flops 512 | bytes 4096 | tf_op jit(solution)/shard_map/convert_element_type | solution.py:192
  13.4 0.1 convert_element_type.138
  13.5 0.7 %convert_element_type.141 = f32[512]{0:T(512)S(1)} convert(s32[512]{0:T(512)} %param.21) | non-fusion elementwise | flops 512 | bytes 4096 | tf_op jit(solution)/shard_map/convert_element_type | solution.py:192
  14.2 0.1 convert_element_type.142
  14.3 0.7 %convert_element_type.149 = f32[512]{0:T(512)S(1)} convert(s32[512]{0:T(512)} %param.22) | non-fusion elementwise | flops 512 | bytes 4096 | tf_op jit(solution)/shard_map/convert_element_type | solution.py:192
  15.0 0.1 convert_element_type.150
  15.0 0.1 convert_reduce_fusion.1
  15.2 0.1 copy.28
  15.3 0.1 convert_element_type.152
  15.4 0.1 copy.25
  15.5 0.1 convert_element_type.144
  15.5 0.9 %convolution_convert_fusion.4 = bf16[64,8,16]{0,2,1:T(8,128)(2,1)S(1)} fusion(bf16[8,8,16]{2,1,0:T(8,128)(2,1)} %param.23, s32[64]{0:T(128)S(1)} %convert_element_type.144), kind=kOutput, calls=%fused_computation.6 | convolution fusion | flops 139776 | bytes 18688 | tf_op jit(solution)/shard_map/mk,kys->mys/dot_general | solution.py:227
  16.5 0.1 copy.27
  16.6 0.1 copy.23
  16.7 0.1 add.23
  16.8 0.1 copy.24
  16.9 0.1 gt.15
  17.0 0.7 %reshape.141 = bf16[32,27]{0,1:T(8,128)(2,1)S(1)} reshape(bf16[32,1,3,3,3]{0,4,3,2,1:T(4,128)(2,1)} %param.25) | data formatting | bytes 3456 | tf_op jit(solution)/shard_map/reshape | solution.py:129
  17.7 0.0 copy-done.2
  17.7 0.0 copy-done.1
  17.7 0.1 maximum_bitcast_fusion
  17.8 0.0 copy-done.3
  17.9 0.2 convolution_convert_fusion.3
  18.1 0.0 copy-done
  18.1 0.8 %convolution_convert_fusion.1 = bf16[64,128,128]{2,0,1:T(8,128)(2,1)S(1)} fusion(bf16[8,128,128]{2,1,0:T(8,128)(2,1)S(1)} %copy-done, s32[64]{0:T(128)S(1)} %convert_element_type.152), kind=kOutput, calls=%fused_computation.3 | convolution fusion | flops 17826304 | bytes 2359552 | tf_op jit(solution)/shard_map/mk,ksp->msp/dot_general | solution.py:236
  18.8 0.0 copy-start.4
  18.8 0.0 copy-start.5
  18.9 0.0 copy-start.6
  18.9 1.1 %all-to-all-done = bf16[16,4,2048]{2,1,0:T(4,128)(2,1)S(1)} async-done(((bf16[16,4,2048]{2,1,0:T(4,128)(2,1)}), bf16[16,4,2048]{2,1,0:T(4,128)(2,1)S(1)}, u32[]{:S(2)}, u32[]{:S(2)}) %all-to-all-start) | async-done | bytes 262176 | tf_op jit(solution)/shard_map/all_to_all | solution.py:221
  19.9 0.2 reshape.139
  20.1 1.9 %fusion = f32[64,8,128]{2,1,0:T(8,128)S(1)} fusion(bf16[64,128,128]{2,0,1:T(8,128)(2,1)S(1)} %convolution_convert_fusion.1, bf16[64,8,16]{2,1,0:T(8,128)(2,1)S(1)} %copy.27, bf16[64,16,128]{2,1,0:T(8,128)(2,1)S(1)} %reshape.139), kind=kOutput, calls=%fused_computation.1 | convolution fusion | flops 18939904 | bytes 2637824 | tf_op jit(solution)/shard_map/myw,mwp->myp/dot_general | solution.py:239
  22.0 0.2 convolution_convert_fusion.5
  22.3 3.7 %collective-permute-start = (bf16[1,4,3,512]{3,1,2,0:T(4,128)(2,1)S(1)}, bf16[1,4,3,512]{3,1,2,0:T(4,128)(2,1)S(1)}, u32[]{:S(2)}, u32[]{:S(2)}) collective-permute-start(bf16[1,4,3,512]{3,1,2,0:T(4,128)(2,1)S(1)} %get-tuple-element.10), channel_id=1, source_target_pairs={{0,1},{1,2},{2,3},{3,4},{4,5},{5,6},{6,7},{7,8},{8,9},{9,10},{10,1... | collective-permute-start | bytes 36872 | tf_op jit(solution)/shard_map/ppermute | solution.py:23
  26.0 1.9 %collective-permute-start.1 = (bf16[1,4,3,512]{3,1,2,0:T(4,128)(2,1)S(1)}, bf16[1,4,3,512]{3,1,2,0:T(4,128)(2,1)S(1)}, u32[]{:S(2)}, u32[]{:S(2)}) collective-permute-start(bf16[1,4,3,512]{3,1,2,0:T(4,128)(2,1)S(1)} %get-tuple-element.11), channel_id=1, source_target_pairs={{1,0},{2,1},{3,2},{4,3},{5,4},{6,5},{7,6},{8,7},{9,8},{10,9},{11,1... | collective-permute-start | bytes 36872 | tf_op jit(solution)/shard_map/ppermute | solution.py:25
  27.9 0.0 copy-done.4
  27.9 0.0 copy-done.5
  27.9 0.0 copy-done.6
  28.0 0.3 copy.37
  28.3 0.3 pad.4.clone
  28.6 0.3 reshape.143.band_ref
  29.0 0.1 copy.34
  29.0 0.0 collective-permute-done
  29.0 2.9 %collective-permute-done.1 = bf16[1,4,3,512]{3,1,2,0:T(4,128)(2,1)S(1)} collective-permute-done((bf16[1,4,3,512]{3,1,2,0:T(4,128)(2,1)S(1)}, bf16[1,4,3,512]{3,1,2,0:T(4,128)(2,1)S(1)}, u32[]{:S(2)}, u32[]{:S(2)}) %collective-permute-start.1) | collective-permute-done | bytes 12320 | tf_op jit(solution)/shard_map/ppermute | solution.py:25
  32.0 8.0 %network.1 = bf16[32,4,8,512]{3,2,1,0:T(8,128)(2,1)} custom-call(bf16[56,512]{1,0:T(8,128)(2,1)S(1)} %reshape.140.image_ref, bf16[256,48]{1,0:T(8,128)(2,1)S(1)} %bitcast.47, bf16[2,288,128]{2,1,0:T(8,128)(2,1)S(1)} %reshape.143.band_ref, f32[256,3]{1,0:T(8,128)S(1)} %bitcast.46), custom_call_target="tpu_custom_call" | custom-call | tf_op jit(solution)/shard_map/network/pallas_call | solution.py:139
  (13 shorter events, 0.2 us)
Async XLA Ops:
  0.0 18.1 %copy-start = (bf16[8,128,128]{2,1,0:T(8,128)(2,1)S(1)}, bf16[8,128,128]{2,1,0:T(8,128)(2,1)}, u32[]{:S(2)}) copy-start(bf16[8,128,128]{2,1,0:T(8,128)(2,1)} %param.24) | copy-start | bytes 786436
  0.0 17.8 %copy-start.3 = (bf16[27,8,48]{2,0,1:T(8,128)(2,1)S(1)}, bf16[27,8,48]{2,0,1:T(8,128)(2,1)}, u32[]{:S(2)}) copy-start(bf16[27,8,48]{2,0,1:T(8,128)(2,1)} %constant.30.clone) | copy-start | bytes 62212
  0.0 17.7 %copy-start.2 = (bf16[32,32,3,3,3]{1,0,4,3,2:T(8,128)(2,1)S(1)}, bf16[32,32,3,3,3]{1,0,4,3,2:T(8,128)(2,1)}, u32[]{:S(2)}) copy-start(bf16[32,32,3,3,3]{1,0,4,3,2:T(8,128)(2,1)} %param.27) | copy-start | bytes 165892
  0.0 17.7 %copy-start.1 = (bf16[32,32,3,3,3]{1,0,4,3,2:T(8,128)(2,1)S(1)}, bf16[32,32,3,3,3]{1,0,4,3,2:T(8,128)(2,1)}, u32[]{:S(2)}) copy-start(bf16[32,32,3,3,3]{1,0,4,3,2:T(8,128)(2,1)} %param.29) | copy-start | bytes 165892
  5.4 14.5 %all-to-all-start = ((bf16[16,4,2048]{2,1,0:T(4,128)(2,1)}), bf16[16,4,2048]{2,1,0:T(4,128)(2,1)S(1)}, u32[]{:S(2)}, u32[]{:S(2)}) async-start(bf16[16,4,2048]{2,1,0:T(4,128)(2,1)} %reshape.138), calls=%async_computation | async-start | bytes 524288 | tf_op jit(solution)/shard_map/all_to_all | solution.py:221
  18.8 9.1 %copy-start.4 = (f32[32]{0:T(128)S(1)}, f32[32]{0:T(128)}, u32[]{:S(2)}) copy-start(f32[32]{0:T(128)} %param.30) | copy-start | bytes 388
  18.8 9.1 %copy-start.5 = (f32[32]{0:T(128)S(1)}, f32[32]{0:T(128)}, u32[]{:S(2)}) copy-start(f32[32]{0:T(128)} %param.28) | copy-start | bytes 388
  18.9 9.1 %copy-start.6 = (f32[32]{0:T(128)S(1)}, f32[32]{0:T(128)}, u32[]{:S(2)}) copy-start(f32[32]{0:T(128)} %param.26) | copy-start | bytes 388
  22.3 6.7 %collective-permute-start = (bf16[1,4,3,512]{3,1,2,0:T(4,128)(2,1)S(1)}, bf16[1,4,3,512]{3,1,2,0:T(4,128)(2,1)S(1)}, u32[]{:S(2)}, u32[]{:S(2)}) collective-permute-start(bf16[1,4,3,512]{3,1,2,0:T(4,128)(2,1)S(1)} %get-tuple-element.10), channel_id=1, source_target_pairs={{0,1},{1,2},{2,3},{3,4},{4,5},{5,6},{6,7},{7,8},{8,9},{9,10},{10,1... | collective-permute-start | bytes 36872 | tf_op jit(solution)/shard_map/ppermute | solution.py:23
  26.0 5.9 %collective-permute-start.1 = (bf16[1,4,3,512]{3,1,2,0:T(4,128)(2,1)S(1)}, bf16[1,4,3,512]{3,1,2,0:T(4,128)(2,1)S(1)}, u32[]{:S(2)}, u32[]{:S(2)}) collective-permute-start(bf16[1,4,3,512]{3,1,2,0:T(4,128)(2,1)S(1)} %get-tuple-element.11), channel_id=1, source_target_pairs={{1,0},{2,1},{3,2},{4,3},{5,4},{6,5},{7,6},{8,7},{9,8},{10,9},{11,1... | collective-permute-start | bytes 36872 | tf_op jit(solution)/shard_map/ppermute | solution.py:25

commit v2 on v1

--- a/solution.py
+++ b/solution.py
@@ -10,23 +10,226 @@
 YB = 8
 Z = 4
 CAP = 4
-
-
-def with_halo(cells, sides, width):
-    for axis, dim in sides:
-        count = lax.axis_size(axis)
-        ends = count - 1
-        head = lax.slice_in_dim(cells, 0, width, axis=dim)
-        tail = lax.slice_in_dim(cells, cells.shape[dim] - width, cells.shape[dim], axis=dim)
-        cells = jnp.concatenate(
+HALO = 3
+
+
+MESH = pl.DeviceIdType.MESH
+GROUP = 4
+NT = (((1,), (1,)), ((), ()))
+
+
+def message_row(line):
+    own, before = line < CAP * YB, line < CAP * (YB + HALO)
+    side = jnp.where(before, line - CAP * YB, line - CAP * (YB + HALO))
+    offset = jnp.where(own, 0, jnp.where(before, -1, 1))
+    slot = jnp.where(own, line // YB, side // HALO)
+    rest = jnp.where(own, line % YB, side % HALO)
+    row = jnp.where(own | ~before, rest, rest + YB - HALO)
+    used = line < CAP * (YB + 2 * HALO)
+    return jnp.where(used, offset * CAP + slot, -1000), row, row + offset * YB + HALO
+
+
+def iota(shape, axis):
+    return lax.broadcasted_iota(jnp.int32, shape, axis)
+
+
+def onehot(mask):
+    return jnp.where(mask, 1.0, 0.0).astype(jnp.bfloat16)
+
+
+def render(
+    tiles_ref, dest_ref, tile_ref, z_ref, xb_ref, ky_ref, kx_ref, wy_ref, wx_ref, image_ref,
+    fields, sent, arrived, send_sem, recv_sem,
+):
+    count = lax.axis_size("gy")
+    own_index = lax.axis_index("gy")
+    lines = sent.shape[1]
+    live = CAP * (YB + 2 * HALO)
+    lanes = dest_ref.shape[1]
+    per_device = dest_ref.shape[0] * lanes // count
+    window = YB + 2 * HALO
+    order = sorted(range(1, count), key=lambda i: -min(i, count - i))
+
+    arrived[:, live - live % 16 :, :] = jnp.zeros(
+        (count, lines - live + live % 16, arrived.shape[2]), jnp.bfloat16
+    )
+    barrier = pltpu.get_barrier_semaphore()
+    for i in order:
+        pl.semaphore_signal(
+            barrier, inc=1, device_id={"gy": lax.rem(own_index + i, count)}, device_id_type=MESH
+        )
+
+    dest = dest_ref[...]
+    place = iota(dest.shape, 1) % per_device
+    rank = jnp.zeros_like(dest)
+    for step in range(1, per_device):
+        same = (pltpu.roll(dest, step, 1) == dest) & (place >= step)
+        rank = rank + jnp.where(same, 1, 0)
+    rows = [
+        dest * CAP + rank,
+        ky_ref[...],
+        tile_ref[...],
+        kx_ref[...] + 1,
+        xb_ref[...] * (window * Z) + z_ref[...] + 1,
+    ]
+    rows = [row.astype(jnp.float32) for row in rows]
+    rows = rows + [jnp.zeros_like(rows[0])] * 3
+    span = GROUP * per_device // lanes
+    for group in range(count // GROUP):
+        for part in range(span):
+            line = group * span + part
+            fields[group, :, part * lanes : (part + 1) * lanes] = jnp.concatenate(
+                [row[line : line + 1] for row in rows], axis=0
+            )
+
+    own_group = own_index // GROUP
+    mine = fields[own_group].astype(jnp.bfloat16)
+    samples = per_device * YB
+    expand = onehot(
+        iota((samples, GROUP * per_device), 1)
+        == iota((samples, GROUP * per_device), 0) // YB + (own_index % GROUP) * per_device
+    )
+    column = lax.dot_general(expand, mine, NT, preferred_element_type=jnp.float32)
+    along = lax.dot_general(mine, expand, NT, preferred_element_type=jnp.float32)
+    blocks, tile_rows = wy_ref.shape
+    spot = iota((samples, blocks), 1)
+    picked = onehot(
+        ((spot // YB).astype(jnp.float32) == column[:, 1:2])
+        & (spot % YB == iota((samples, blocks), 0) % YB)
+    )
+    vertical = jnp.dot(picked, wy_ref[...], preferred_element_type=jnp.float32)
+    pixels = tiles_ref.shape[0]
+    repeat = onehot(iota((tile_rows, pixels), 1) % tile_rows == iota((tile_rows, pixels), 0))
+    vertical = jnp.dot(
+        vertical.astype(jnp.bfloat16), repeat, preferred_element_type=jnp.float32
+    )
+    chosen = (iota((samples, pixels), 1) // tile_rows).astype(jnp.float32) == column[:, 2:3]
+    vertical = jnp.where(chosen, vertical, 0.0).astype(jnp.bfloat16)
+    row_samples = jnp.dot(
+        vertical, tiles_ref[...], preferred_element_type=jnp.float32
+    ).astype(jnp.bfloat16)
+
+    key, row, _ = message_row(iota((lines, samples), 0))
+    wanted = along[0:1, :] - key.astype(jnp.float32)
+    wanted = jnp.where(row == iota((lines, samples), 1) % YB, wanted, -4000.0)
+
+    def message(number):
+        target = lax.rem(own_index + number, count)
+        return onehot(wanted == (target * CAP).astype(jnp.float32))
+
+    copies = []
+    order = order + [0]
+    for start in range(0, count, GROUP):
+        numbers = order[start : start + GROUP]
+        packed = jnp.dot(
+            jnp.concatenate([message(number) for number in numbers], axis=0),
+            row_samples,
+            preferred_element_type=jnp.float32,
+        ).astype(jnp.bfloat16)
+        for part, number in enumerate(numbers):
+            block = packed[part * lines : (part + 1) * lines]
+            if number == 0:
+                arrived[own_index] = block
+            else:
+                sent[number] = block
+        if start == 0:
+            pl.semaphore_wait(barrier, count - 1)
+        for number in numbers:
+            if number > 0:
+                copy = pltpu.make_async_remote_copy(
+                    src_ref=sent.at[number, 0:live],
+                    dst_ref=arrived.at[own_index, 0:live],
+                    send_sem=send_sem.at[number],
+                    recv_sem=recv_sem.at[number],
+                    device_id={"gy": lax.rem(own_index + number, count)},
+                    device_id_type=MESH,
+                )
+                copy.start()
+                copies.append(copy)
+
+    depth = GROUP * lines
+    entries = GROUP * per_device
+    total = None
+    horizontals = wx_ref.shape[0] // wx_ref.shape[1]
+    key, _, window_row = message_row(iota((depth, entries), 0) % lines)
+    sources = iota((depth, entries), 0) // lines == iota((depth, entries), 1) // per_device
+    wanted_key = jnp.where(sources, key + own_index * CAP, -5000).astype(jnp.float32)
+    _, _, target_row = message_row(iota((1, depth), 1) % lines)
+    x_blocks = image_ref.shape[1] // wx_ref.shape[1]
+    targets = x_blocks * window * Z
+    meta = []
+    for group in range(count // GROUP):
+        held = fields[group]
+        match = onehot(held[0:1, :] == wanted_key)
+        held = held.astype(jnp.bfloat16)
+        source = lax.dot_general(match, held, NT, preferred_element_type=jnp.float32)
+        target = lax.dot_general(held, match, NT, preferred_element_type=jnp.float32)
+        code = target[4:5, :]
+        code = jnp.where(
+            code > 0.5, code - 1.0 + (target_row * Z).astype(jnp.float32), -1.0
+        )
+        placed = onehot(iota((targets, depth), 0).astype(jnp.float32) == code)
+        meta.append((source[:, 3:4], placed))
+    for copy in copies:
+        copy.wait()
+    for group in range(count // GROUP):
+        horizontal, placed = meta[group]
+        samples_in = jnp.concatenate(
+            [arrived[group * GROUP + part] for part in range(GROUP)], axis=0
+        ).astype(jnp.float32)
+        spread = jnp.concatenate(
             [
-                lax.ppermute(tail, axis, [(i, (i + 1) % count) for i in range(ends)]),
-                cells,
-                lax.ppermute(head, axis, [((i + 1) % count, i) for i in range(ends)]),
+                jnp.where(horizontal == float(block + 1), samples_in, 0.0).astype(jnp.bfloat16)
+                for block in range(horizontals)
             ],
-            axis=dim,
-        )
-    return cells
+            axis=1,
+        )
+        patches = jnp.dot(spread, wx_ref[...], preferred_element_type=jnp.float32)
+        high = patches.astype(jnp.bfloat16)
+        rest = patches - high.astype(jnp.float32)
+        middle = rest.astype(jnp.bfloat16)
+        low = (rest - middle.astype(jnp.float32)).astype(jnp.bfloat16)
+        part = jnp.dot(
+            placed, jnp.concatenate([high, middle, low], axis=1), preferred_element_type=jnp.float32
+        )
+        total = part if total is None else total + part
+    columns = wx_ref.shape[1]
+    total = total[:, :columns] + total[:, columns : 2 * columns] + total[:, 2 * columns :]
+    for block in range(x_blocks):
+        image_ref[:, block * columns : (block + 1) * columns] = total[
+            block * window * Z : (block + 1) * window * Z
+        ].astype(jnp.bfloat16)
+
+
+def rendered_window(tiles, entries, wy_table, wx_table):
+    count = lax.axis_size("gy")
+    tiles_dev, tile_rows, tile_cols = tiles.shape
+    lines = -(-CAP * (YB + 2 * HALO) // 16) * 16
+    per_device = entries[0].size // count
+    entries = [entry.reshape(-1, 128) for entry in entries]
+    vmem = pl.BlockSpec(memory_space=pltpu.VMEM)
+    return pl.pallas_call(
+        render,
+        out_shape=jax.ShapeDtypeStruct(((YB + 2 * HALO) * Z, X), jnp.bfloat16),
+        in_specs=[vmem] * 9,
+        out_specs=vmem,
+        scratch_shapes=[
+            pltpu.VMEM((count // GROUP, 8, GROUP * per_device), jnp.float32),
+            pltpu.VMEM((count, lines, tile_cols), jnp.bfloat16),
+            pltpu.VMEM((count, lines, tile_cols), jnp.bfloat16),
+            pltpu.SemaphoreType.DMA((count,)),
+            pltpu.SemaphoreType.DMA((count,)),
+        ],
+        compiler_params=pltpu.CompilerParams(
+            collective_id=0, has_side_effects=True, vmem_limit_bytes=48 << 20
+        ),
+        name="render",
+    )(
+        tiles.reshape(tiles_dev * tile_rows, tile_cols),
+        *entries,
+        wy_table.reshape(-1, tile_rows),
+        wx_table.reshape(-1, tile_cols),
+    )
 
 
 def first_taps():
@@ -169,92 +372,12 @@
     w_third,
     b_third,
 ):
-    devices_gy = lax.axis_size("gy")
-    own_index = lax.axis_index("gy")
-    tiles_dev, tile_rows, tile_cols = tiles.shape
-    per_device = entry_dest.shape[0] // devices_gy
-    slot_total = devices_gy * CAP
-    target_brick = entry_dest[:, 0].reshape(devices_gy, per_device)
-    later_pos = lax.broadcasted_iota(jnp.int32, (per_device, per_device), 0)
-    earlier_pos = lax.broadcasted_iota(jnp.int32, (per_device, per_device), 1)
-    same_brick = (target_brick[:, :, None] == target_brick[:, None, :]) & (earlier_pos < later_pos)[
-        None
-    ]
-    slot_rank = jnp.sum(same_brick, axis=2, dtype=jnp.int32)
-    capacity_iota = lax.broadcasted_iota(jnp.int32, (1, CAP, 1), 1)
-    matched = (
-        (target_brick == own_index)[:, None, :] & (slot_rank[:, None, :] == capacity_iota)
-    ).astype(jnp.float32)
-    slot_live = jnp.sum(matched, axis=2).reshape(-1) > 0.5
-
-    def slot_field(field):
-        return (
-            jnp.sum(matched * field.reshape(devices_gy, 1, per_device).astype(jnp.float32), axis=2)
-            .reshape(-1)
-            .astype(jnp.int32)
-        )
-
-    slot_z = slot_field(entry_z)
-    slot_xb = slot_field(entry_xb)
-    slot_ky = slot_field(entry_ky)
-    slot_kx = slot_field(entry_kx)
-    local_tiles = tiles.reshape(tiles_dev, tile_rows * tile_cols)
-    own_brick = lax.dynamic_index_in_dim(target_brick, own_index, 0, keepdims=False)
-    own_rank = lax.dynamic_index_in_dim(slot_rank, own_index, 0, keepdims=False)
-    own_tile = lax.dynamic_index_in_dim(
-        entry_tile.reshape(devices_gy, per_device), own_index, 0, keepdims=False
-    )
-    slot_target = own_brick * CAP + own_rank
-    chooser = (
-        lax.broadcasted_iota(jnp.int32, (slot_total, per_device), 0) == slot_target[None, :]
-    ).astype(jnp.bfloat16)
-    tile_choice = (
-        own_tile[:, None] == lax.broadcasted_iota(jnp.int32, (per_device, tiles_dev), 1)
-    ).astype(jnp.bfloat16)
-    pick_matrix = jnp.dot(chooser, tile_choice, preferred_element_type=jnp.float32).astype(
-        jnp.bfloat16
-    )
-    send_buffer = jnp.dot(pick_matrix, local_tiles, preferred_element_type=jnp.float32).astype(
-        jnp.bfloat16
-    )
-    send_buffer = send_buffer.reshape(devices_gy, CAP, tile_rows * tile_cols)
-    arrived = lax.all_to_all(send_buffer, "gy", split_axis=0, concat_axis=0, tiled=True).reshape(
-        slot_total, tile_rows, tile_cols
-    )
-    ky_onehot = (
-        slot_ky[:, None] == lax.broadcasted_iota(jnp.int32, (1, wy_table.shape[0]), 1)
-    ).astype(jnp.bfloat16)
-    vertical = jnp.einsum(
-        "mk,kys->mys", ky_onehot, wy_table, preferred_element_type=jnp.float32
-    ).astype(jnp.bfloat16)
-    row_samples = jnp.einsum(
-        "mys,msw->myw", vertical, arrived, preferred_element_type=jnp.float32
-    ).astype(jnp.bfloat16)
-    kx_onehot = (
-        slot_kx[:, None] == lax.broadcasted_iota(jnp.int32, (1, wx_table.shape[0]), 1)
-    ).astype(jnp.bfloat16)
-    horizontal = jnp.einsum(
-        "mk,ksp->msp", kx_onehot, wx_table, preferred_element_type=jnp.float32
-    ).astype(jnp.bfloat16)
-    patches = jnp.einsum(
-        "myw,mwp->myp", row_samples, horizontal, preferred_element_type=jnp.float32
-    )
-    x_blocks = X // tile_cols
-    placement = (
-        (slot_z * x_blocks + slot_xb)[:, None]
-        == lax.broadcasted_iota(jnp.int32, (1, Z * x_blocks), 1)
-    ) & slot_live[:, None]
-    rendered = jnp.einsum(
-        "mq,myp->qyp", placement.astype(jnp.float32), patches, precision=lax.Precision.HIGHEST
-    )
-    image = (
-        rendered.reshape(Z, x_blocks, YB, tile_cols)
-        .transpose(0, 2, 1, 3)
-        .reshape(Z, YB, X)
-        .astype(jnp.bfloat16)
-    )
-    extended = with_halo(image[None], (("gy", 2),), 3)
-    rows = extended[0].transpose(1, 0, 2).reshape((YB + 6) * Z, X)
+    rows = rendered_window(
+        tiles,
+        (entry_dest, entry_tile, entry_z, entry_xb, entry_ky, entry_kx),
+        wy_table,
+        wx_table,
+    )
     return network(rows, w_first, b_first, w_second, b_second, w_third, b_third)
 
 

time: 40.6 us -> 26.1 us (0.64)
  the two profiles are of different devices: /device:TPU:15 before, /device:TPU:0 now
where the time goes in v2:
time: 26.1 us; the launch traced here: 25.9 us
  Pallas kernels  21.8 us (84%)
  local copies, waits for them, and re-layouts  2.07 us (8%)
  matrix products  1.1 us (4%)
  other arithmetic  0.84 us (3%)
    pallas_call x1, Pallas kernels, rendered_window(): pl.pallas_call(render, out_shape=jax.ShapeDtypeStruct(((YB + 2 * HALO) *...  13.8 us
    pallas_call x1, Pallas kernels, network(): pl.pallas_call(convolutions, out_shape=jax.ShapeDtypeStruct((channels, Z,...  7.97 us
    unnamed x25, local copies, waits for them, and re-layouts  1.3 us
    dot_general x1, matrix products, network(): jnp.einsum('ot,trk->rok', w_first.reshape(channels, 27), first_taps().ast...  1.1 us
    another operation x1, other arithmetic, network(): jnp.stack([b_first, b_second, b_third], axis=1)  0.73 us

profile of v2, /device:TPU:0, one launch (start us, length us, event | category | flops | bytes accessed | tf_op | source)
XLA Modules:
  0.0 25.9 jit_solution(12798271089854333210)
XLA Ops:
  0.0 0.0 copy-start.11
  0.0 0.0 copy-start.1
  0.0 0.7 %pad_maximum_fusion = f32[32,3]{0,1:T(4,128)S(1)} fusion(f32[32,1]{0,1:T(1,128)} %bitcast.39, f32[32,1]{0,1:T(1,128)} %bitcast.40, f32[32,1]{0,1:T(1,128)} %bitcast.41), kind=kLoop, calls=%fused_computation.3 | loop fusion | flops 192 | bytes 768 | tf_op jit(solution)/shard_map/stack | solution.py:340
  0.7 0.0 copy-done.11
  0.8 0.1 copy.19
  0.8 0.0 copy-start.2
  0.9 0.0 copy-start.3
  0.9 0.0 copy-start.4
  0.9 0.0 copy-start.5
  0.9 0.0 copy-start.6
  0.9 0.0 copy-start.7
  0.9 0.0 copy-start.8
  0.9 1.1 %convolution_convert_fusion = bf16[8,48,32]{1,2,0:T(8,128)(2,1)S(1)} fusion(bf16[27,8,48]{2,0,1:T(8,128)(2,1)} %constant.5.clone, bf16[32,27]{0,1:T(8,128)(2,1)S(1)} %reshape.49), kind=kOutput, calls=%fused_computation | convolution fusion | flops 675840 | bytes 47040 | tf_op jit(solution)/shard_map/ot,trk->rok/dot_general | solution.py:330
  2.0 0.0 copy-done.1
  2.0 0.0 copy-done.2
  2.0 0.0 copy-done.3
  2.0 0.0 copy-done.4
  2.0 0.0 copy-done.5
  2.0 0.0 copy-done.6
  2.1 0.0 copy-done.7
  2.1 0.0 copy-done.8
  2.1 0.0 copy-start
  2.1 0.9 %copy-done = bf16[8,128,128]{2,1,0:T(8,128)(2,1)S(1)} copy-done((bf16[8,128,128]{2,1,0:T(8,128)(2,1)S(1)}, bf16[8,128,128]{2,1,0:T(8,128)(2,1)}, u32[]{:S(2)}) %copy-start) | copy-done | bytes 262168
  3.0 0.0 copy-start.9
  3.0 0.0 copy-start.10
  3.0 13.8 %render.1.image_ref = bf16[56,512]{1,0:T(8,128)(2,1)S(1)} custom-call(bf16[512,128]{1,0:T(8,128)(2,1)S(1)} %bitcast.29, s32[4,128]{1,0:T(4,128)S(1)} %bitcast.31, s32[4,128]{1,0:T(4,128)S(1)} %bitcast.32, s32[4,128]{1,0:T(4,128)S(1)} %bitcast.33, s32[4,128]{1,0:T(4,128)S(1)} %bitcast.34, s32[4,128]{1,0:T(4,128)S(1)} %bitcast.35, s32[4,128]{1,0:T(4,128)S(1)} %bitcast.36, ...), custom_call_target="tpu_custom_call" | custom-call | tf_op jit(solution)/shard_map/render/pallas_call | solution.py:211
  16.9 0.0 copy-done.9
  16.9 0.0 copy-done.10
  16.9 0.1 maximum_bitcast_fusion
  17.0 0.3 %copy.22 = bf16[2,3,3,32,3,32]{5,4,3,2,1,0:T(4,128)(2,1)S(1)} copy(bf16[2,3,3,32,3,32]{5,3,1,2,4,0:T(8,128)(2,1)S(1)} %maximum_bitcast_fusion) | data formatting | bytes 221184
  17.3 0.3 %pad.4.clone = bf16[2,3,3,32,4,32]{5,4,3,2,1,0:T(4,128)(2,1)S(1)} pad(bf16[2,3,3,32,3,32]{5,4,3,2,1,0:T(4,128)(2,1)S(1)} %copy.22, bf16[]{:T(256)} %constant.4.clone.1), padding=0_0x0_0x0_0x0_0x0_1x0_0 | pad | bytes 258050 | tf_op jit(solution)/shard_map/jit(_pad)/pad | solution.py:338
  17.7 0.3 %reshape.51.band_ref = bf16[2,288,128]{2,1,0:T(8,128)(2,1)S(1)} reshape(bf16[2,3,3,32,4,32]{5,4,3,2,1,0:T(4,128)(2,1)S(1)} %pad.4.clone) | data formatting | bytes 294912 | tf_op jit(solution)/shard_map/reshape | solution.py:339
  18.0 8.0 %network.1 = bf16[32,4,8,512]{3,2,1,0:T(8,128)(2,1)} custom-call(bf16[56,512]{1,0:T(8,128)(2,1)S(1)} %render.1.image_ref, bf16[256,48]{1,0:T(8,128)(2,1)S(1)} %bitcast.27, bf16[2,288,128]{2,1,0:T(8,128)(2,1)S(1)} %reshape.51.band_ref, f32[256,3]{1,0:T(8,128)S(1)} %bitcast.26), custom_call_target="tpu_custom_call" | custom-call | tf_op jit(solution)/shard_map/network/pallas_call | solution.py:342
  (2 shorter events, 0.0 us)
Async XLA Ops:
  0.0 0.7 %copy-start.11 = (bf16[32,1,3,3,3]{0,4,3,2,1:T(4,128)(2,1)S(1)}, bf16[32,1,3,3,3]{0,4,3,2,1:T(4,128)(2,1)}, u32[]{:S(2)}) copy-start(bf16[32,1,3,3,3]{0,4,3,2,1:T(4,128)(2,1)} %param.25) | copy-start | bytes 5188
  0.0 2.0 %copy-start.1 = (bf16[32,16,128]{2,1,0:T(8,128)(2,1)S(1)}, bf16[32,16,128]{2,1,0:T(8,128)(2,1)}, u32[]{:S(2)}) copy-start(bf16[32,16,128]{2,1,0:T(8,128)(2,1)} %param.16) | copy-start | bytes 393220
  0.8 1.2 %copy-start.2 = (bf16[8,8,16]{2,1,0:T(8,128)(2,1)S(1)}, bf16[8,8,16]{2,1,0:T(8,128)(2,1)}, u32[]{:S(2)}) copy-start(bf16[8,8,16]{2,1,0:T(8,128)(2,1)} %param.23) | copy-start | bytes 6148
  0.9 1.2 %copy-start.3 = (s32[512,1]{0,1:T(1,128)S(1)}, s32[512,1]{0,1:T(1,128)}, u32[]{:S(2)}) copy-start(s32[512,1]{0,1:T(1,128)} %param.17) | copy-start | bytes 6148
  0.9 1.2 %copy-start.4 = (s32[512]{0:T(512)S(1)}, s32[512]{0:T(512)}, u32[]{:S(2)}) copy-start(s32[512]{0:T(512)} %param.18) | copy-start | bytes 6148
  0.9 1.2 %copy-start.5 = (s32[512]{0:T(512)S(1)}, s32[512]{0:T(512)}, u32[]{:S(2)}) copy-start(s32[512]{0:T(512)} %param.19) | copy-start | bytes 6148
  0.9 1.2 %copy-start.6 = (s32[512]{0:T(512)S(1)}, s32[512]{0:T(512)}, u32[]{:S(2)}) copy-start(s32[512]{0:T(512)} %param.20) | copy-start | bytes 6148
  0.9 1.2 %copy-start.7 = (s32[512]{0:T(512)S(1)}, s32[512]{0:T(512)}, u32[]{:S(2)}) copy-start(s32[512]{0:T(512)} %param.21) | copy-start | bytes 6148
  0.9 1.2 %copy-start.8 = (s32[512]{0:T(512)S(1)}, s32[512]{0:T(512)}, u32[]{:S(2)}) copy-start(s32[512]{0:T(512)} %param.22) | copy-start | bytes 6148
  2.1 1.0 %copy-start = (bf16[8,128,128]{2,1,0:T(8,128)(2,1)S(1)}, bf16[8,128,128]{2,1,0:T(8,128)(2,1)}, u32[]{:S(2)}) copy-start(bf16[8,128,128]{2,1,0:T(8,128)(2,1)} %param.24) | copy-start | bytes 786436
  3.0 13.8 %copy-start.9 = (bf16[32,32,3,3,3]{1,0,4,3,2:T(8,128)(2,1)S(1)}, bf16[32,32,3,3,3]{1,0,4,3,2:T(8,128)(2,1)}, u32[]{:S(2)}) copy-start(bf16[32,32,3,3,3]{1,0,4,3,2:T(8,128)(2,1)} %param.29) | copy-start | bytes 165892
  3.0 13.8 %copy-start.10 = (bf16[32,32,3,3,3]{1,0,4,3,2:T(8,128)(2,1)S(1)}, bf16[32,32,3,3,3]{1,0,4,3,2:T(8,128)(2,1)}, u32[]{:S(2)}) copy-start(bf16[32,32,3,3,3]{1,0,4,3,2:T(8,128)(2,1)} %param.27) | copy-start | bytes 165892

commit v3 on v2

--- a/solution.py
+++ b/solution.py
@@ -37,9 +37,67 @@
     return jnp.where(mask, 1.0, 0.0).astype(jnp.bfloat16)
 
 
+def arrange(spots_ref, w_first_ref, deep, b_first_ref, b_second_ref, b_third_ref, taps_ref, band, bias_ref):
+    channels = b_first_ref.shape[1]
+    plane = Z * channels
+    first = jnp.concatenate(
+        [w_first_ref[k].astype(jnp.float32) for k in range(w_first_ref.shape[0])], axis=0
+    )
+    first = lax.dot_general(
+        first.astype(jnp.bfloat16),
+        spots_ref[...],
+        (((0,), (0,)), ((), ())),
+        preferred_element_type=jnp.float32,
+    ).astype(jnp.bfloat16)
+    for block in range(2 * Z):
+        taps_ref[block * channels : (block + 1) * channels, :] = first[
+            :, block * 128 : (block + 1) * 128
+        ]
+    lane = iota((2 * plane, 128), 1)
+    biases = jnp.zeros((2 * plane, 128), jnp.float32)
+    square = (channels, channels)
+    for layer, b_ref in enumerate((b_first_ref, b_second_ref, b_third_ref)):
+        diagonal = jnp.where(iota(square, 0) == iota(square, 1), b_ref[...], 0.0)
+        column = jnp.sum(diagonal, axis=1, keepdims=True)
+        biases = jnp.where(lane == layer, jnp.concatenate([column] * (2 * Z), axis=0), biases)
+    bias_ref[...] = biases
+    lane = iota((9 * channels, plane), 1)
+    empty = jnp.zeros((channels, plane), jnp.bfloat16)
+    for layer in range(2):
+        source = jnp.concatenate(
+            [
+                jnp.concatenate(
+                    [deep[layer, (a * 3 + b) * 3 + c].astype(jnp.float32) for a in range(3)]
+                    + [jnp.zeros(square, jnp.float32)],
+                    axis=1,
+                )
+                for c in range(3)
+                for b in range(3)
+            ],
+            axis=0,
+        )
+        for zo in range(Z):
+            offset = (zo - 1) * channels
+            placed = source if offset == 0 else pltpu.roll(source, offset % plane, 1)
+            placed = jnp.where((lane >= offset) & (lane < offset + 3 * channels), placed, 0.0)
+            placed = placed.astype(jnp.bfloat16)
+            for c in range(3):
+                for yo in range(2):
+                    rows = (yo * Z + zo) * channels
+                    for yi in range(4):
+                        b = yi - yo
+                        cols = (yi * 3 + c) * plane
+                        block = empty
+                        if 0 <= b < 3:
+                            block = placed[(c * 3 + b) * channels : (c * 3 + b + 1) * channels]
+                        band[layer, rows : rows + channels, cols : cols + plane] = block
+
+
 def render(
-    tiles_ref, dest_ref, tile_ref, z_ref, xb_ref, ky_ref, kx_ref, wy_ref, wx_ref, image_ref,
-    fields, sent, arrived, send_sem, recv_sem,
+    tiles_ref, dest_ref, tile_ref, z_ref, xb_ref, ky_ref, kx_ref, wy_ref, wx_hbm,
+    spots_ref, w_first_ref, w_second_hbm, w_third_hbm, b_first_ref, b_second_ref, b_third_ref,
+    image_ref, taps_ref, band, bias_ref,
+    fields, sent, arrived, wx_ref, deep, send_sem, recv_sem, load_sem,
 ):
     count = lax.axis_size("gy")
     own_index = lax.axis_index("gy")
@@ -50,6 +108,13 @@
     window = YB + 2 * HALO
     order = sorted(range(1, count), key=lambda i: -min(i, count - i))
 
+    loads = [
+        pltpu.make_async_copy(w_second_hbm, deep.at[0], load_sem.at[0]),
+        pltpu.make_async_copy(w_third_hbm, deep.at[1], load_sem.at[1]),
+        pltpu.make_async_copy(wx_hbm, wx_ref, load_sem.at[2]),
+    ]
+    for load in loads:
+        load.start()
     arrived[:, live - live % 16 :, :] = jnp.zeros(
         (count, lines - live + live % 16, arrived.shape[2]), jnp.bfloat16
     )
@@ -170,6 +235,9 @@
         )
         placed = onehot(iota((targets, depth), 0).astype(jnp.float32) == code)
         meta.append((source[:, 3:4], placed))
+    for load in loads:
+        load.wait()
+    arrange(spots_ref, w_first_ref, deep, b_first_ref, b_second_ref, b_third_ref, taps_ref, band, bias_ref)
     for copy in copies:
         copy.wait()
     for group in range(count // GROUP):
@@ -201,24 +269,35 @@
         ].astype(jnp.bfloat16)
 
 
-def rendered_window(tiles, entries, wy_table, wx_table):
+def rendered_window(tiles, entries, wy_table, wx_table, weights, biases):
     count = lax.axis_size("gy")
     tiles_dev, tile_rows, tile_cols = tiles.shape
     lines = -(-CAP * (YB + 2 * HALO) // 16) * 16
     per_device = entries[0].size // count
     entries = [entry.reshape(-1, 128) for entry in entries]
     vmem = pl.BlockSpec(memory_space=pltpu.VMEM)
+    hbm = pl.BlockSpec(memory_space=pl.ANY)
+    channels = biases[0].shape[0]
+    plane = Z * channels
     return pl.pallas_call(
         render,
-        out_shape=jax.ShapeDtypeStruct(((YB + 2 * HALO) * Z, X), jnp.bfloat16),
-        in_specs=[vmem] * 9,
-        out_specs=vmem,
+        out_shape=[
+            jax.ShapeDtypeStruct(((YB + 2 * HALO) * Z, X), jnp.bfloat16),
+            jax.ShapeDtypeStruct((2 * plane, 128), jnp.bfloat16),
+            jax.ShapeDtypeStruct((2, 2 * plane, 12 * plane), jnp.bfloat16),
+            jax.ShapeDtypeStruct((2 * plane, 128), jnp.float32),
+        ],
+        in_specs=[vmem] * 8 + [hbm] + [vmem] * 2 + [hbm] * 2 + [vmem] * 3,
+        out_specs=[vmem] * 4,
         scratch_shapes=[
             pltpu.VMEM((count // GROUP, 8, GROUP * per_device), jnp.float32),
             pltpu.VMEM((count, lines, tile_cols), jnp.bfloat16),
             pltpu.VMEM((count, lines, tile_cols), jnp.bfloat16),
+            pltpu.VMEM((wx_table.shape[0] * wx_table.shape[1], tile_cols), jnp.bfloat16),
+            pltpu.VMEM((2, 27, channels, channels), jnp.bfloat16),
             pltpu.SemaphoreType.DMA((count,)),
             pltpu.SemaphoreType.DMA((count,)),
+            pltpu.SemaphoreType.DMA((3,)),
         ],
         compiler_params=pltpu.CompilerParams(
             collective_id=0, has_side_effects=True, vmem_limit_bytes=48 << 20
@@ -229,6 +308,10 @@
         *entries,
         wy_table.reshape(-1, tile_rows),
         wx_table.reshape(-1, tile_cols),
+        first_taps().astype(jnp.bfloat16),
+        weights[0].transpose(1, 2, 3, 4, 0).reshape(9, 3, channels),
+        *[weight.transpose(2, 3, 4, 0, 1).reshape(27, channels, channels) for weight in weights[1:]],
+        *[bias.reshape(1, channels) for bias in biases],
     )
 
 
@@ -242,7 +325,8 @@
                         zi = zo + a - 1
                         if 0 <= zi < Z:
                             taps[(a * 3 + b) * 3 + c, yo, zo, c, yo + b, zi] = 1.0
-    return taps.reshape(27, 2 * Z, 12 * Z)
+    taps = taps.reshape(27, 2 * Z, 12 * Z)
+    return np.pad(taps, ((0, 0), (0, 0), (0, 128 - 12 * Z))).reshape(27, -1)
 
 
 def shifted(value):
@@ -253,28 +337,11 @@
     return before, value, after
 
 
-def convolutions(image_ref, taps_ref, band_ref, bias_ref, out_ref, band, first, second, third):
+def convolutions(image_ref, taps_ref, band, bias_ref, out_ref, first, second, third):
     own_index = lax.axis_index("gy")
     last_index = lax.axis_size("gy") - 1
     channels = out_ref.shape[0]
     plane = Z * channels
-    lane = lax.broadcasted_iota(jnp.int32, (band_ref.shape[1], plane), 1)
-    band[...] = jnp.zeros_like(band)
-    for layer in range(2):
-        source = band_ref[layer].astype(jnp.float32)
-        for zo in range(Z):
-            offset = (zo - 1) * channels
-            placed = source if offset == 0 else pltpu.roll(source, offset % plane, 1)
-            placed = jnp.where((lane >= offset) & (lane < offset + 3 * channels), placed, 0.0)
-            placed = placed.astype(jnp.bfloat16)
-            for c in range(3):
-                for b in range(3):
-                    block = placed[(c * 3 + b) * channels : (c * 3 + b + 1) * channels]
-                    for yo in range(2):
-                        rows = (yo * Z + zo) * channels
-                        cols = ((yo + b) * 3 + c) * plane
-                        band[layer, rows : rows + channels, cols : cols + plane] = block
-
     def keep(result, target, pair, pairs, extra_rows):
         result = jnp.maximum(result, 0.0)
         for yo in range(2):
@@ -298,46 +365,38 @@
             ],
             axis=0,
         )
-        result = jnp.dot(taps_ref[...], window, preferred_element_type=jnp.float32)
+        result = jnp.dot(taps_ref[:, : 12 * Z], window, preferred_element_type=jnp.float32)
         keep(result + bias_ref[:, 0:1], first, pair, pairs, 2)
     depth = 12 * plane
     for pair in range(YB // 2 + 1):
         window = first[6 * pair * plane : 6 * pair * plane + depth, :]
         result = jnp.dot(band[0], window, preferred_element_type=jnp.float32)
         keep(result + bias_ref[:, 1:2], second, pair, YB // 2 + 1, 1)
-    for pair in range(YB // 2):
-        window = second[6 * pair * plane : 6 * pair * plane + depth, :]
-        result = jnp.dot(band[1], window, preferred_element_type=jnp.float32)
-        result = jnp.maximum(result + bias_ref[:, 2:3], 0.0)
-        for yo in range(2):
-            for zo in range(Z):
-                rows = (yo * Z + zo) * channels
-                start = zo * YB + 2 * pair + yo
-                for block in range(third.shape[0]):
-                    third[block, pl.ds(start, channels, stride=Z * YB), :] = result[
-                        rows : rows + channels, block * 128 : (block + 1) * 128
-                    ]
-    for block in range(third.shape[0]):
-        out_ref[:, :, :, block * 128 : (block + 1) * 128] = (
-            third[block].reshape(channels, Z, YB, 128).astype(jnp.bfloat16)
-        )
-
-
-def network(image, w_first, b_first, w_second, b_second, w_third, b_third):
-    channels = w_first.shape[0]
+    half = min(256, third.shape[0] * 128)
+    for start_x in range(0, third.shape[0] * 128, half):
+        blocks = range(start_x // 128, (start_x + half) // 128)
+        for pair in range(YB // 2):
+            rows = 6 * pair * plane
+            window = second[rows : rows + depth, start_x : start_x + half]
+            result = jnp.dot(band[1], window, preferred_element_type=jnp.float32)
+            result = jnp.maximum(result + bias_ref[:, 2:3], 0.0)
+            for yo in range(2):
+                for zo in range(Z):
+                    rows = (yo * Z + zo) * channels
+                    start = zo * YB + 2 * pair + yo
+                    for part, block in enumerate(blocks):
+                        third[block, pl.ds(start, channels, stride=Z * YB), :] = result[
+                            rows : rows + channels, part * 128 : (part + 1) * 128
+                        ]
+        for block in blocks:
+            out_ref[:, :, :, block * 128 : (block + 1) * 128] = (
+                third[block].reshape(channels, Z, YB, 128).astype(jnp.bfloat16)
+            )
+
+
+def network(image, taps, band, biases, channels):
     width = image.shape[1]
     plane = Z * channels
-    taps = jnp.einsum(
-        "ot,trk->rok",
-        w_first.reshape(channels, 27),
-        first_taps().astype(jnp.bfloat16),
-        preferred_element_type=jnp.float32,
-    )
-    taps = taps.astype(jnp.bfloat16).reshape(2 * plane, 12 * Z)
-    weights = jnp.stack([w_second, w_third]).transpose(0, 5, 4, 1, 3, 2)
-    weights = jnp.pad(weights, ((0, 0), (0, 0), (0, 0), (0, 0), (0, 1), (0, 0)))
-    weights = weights.reshape(2, 9 * channels, 4 * channels)
-    biases = jnp.tile(jnp.stack([b_first, b_second, b_third], axis=1), (2 * Z, 1))
     vmem = pl.BlockSpec(memory_space=pltpu.VMEM)
     return pl.pallas_call(
         convolutions,
@@ -345,14 +404,13 @@
         in_specs=[vmem] * 4,
         out_specs=vmem,
         scratch_shapes=[
-            pltpu.VMEM((2, 2 * plane, 12 * plane), jnp.bfloat16),
             pltpu.VMEM((3 * plane * (YB + 4), width), jnp.bfloat16),
             pltpu.VMEM((3 * plane * (YB + 2), width), jnp.bfloat16),
             pltpu.VMEM((width // 128, plane * YB, 128), jnp.float32),
         ],
         compiler_params=pltpu.CompilerParams(vmem_limit_bytes=48 << 20),
         name="network",
-    )(image, taps, weights, biases)
+    )(image, taps, band, biases)
 
 
 def on_device(
@@ -372,13 +430,15 @@
     w_third,
     b_third,
 ):
-    rows = rendered_window(
+    prepared = rendered_window(
         tiles,
         (entry_dest, entry_tile, entry_z, entry_xb, entry_ky, entry_kx),
         wy_table,
         wx_table,
-    )
-    return network(rows, w_first, b_first, w_second, b_second, w_third, b_third)
+        (w_first, w_second, w_third),
+        (b_first, b_second, b_third),
+    )
+    return network(*prepared, w_first.shape[0])
 
 
 def solution(mesh):

time: 26.1 us -> 34.2 us (1.31); the launches traced: 25.9 us -> 33.7 us
  local copies, waits for them, and re-layouts: 2.07 us -> 12 us
  matrix products: 1.1 us -> 0 us
  other arithmetic: 0.84 us -> 0 us
    unnamed x25 -> x32, local copies, waits for them, and re-layouts: 1.3 us -> 12 us
    dot_general x1 -> x0, matrix products: 1.1 us -> none  [network(): jnp.einsum('ot,trk->rok', w_first.reshape(channels, 27), first_taps().ast...]
    another operation x1 -> x0, other arithmetic: 0.73 us -> none  [network(): jnp.stack([b_first, b_second, b_third], axis=1)]
    pallas_call x1, Pallas kernels: 7.97 us -> 7.25 us  [network(): pl.pallas_call(convolutions, out_shape=jax.ShapeDtypeStruct((channels, Z,...]
    pallas_call x1, Pallas kernels: 13.8 us -> 14.4 us  [rendered_window(): pl.pallas_call(render, out_shape=[jax.ShapeDtypeStruct(((YB + 2 * HALO) *...]
    pad x1 -> x0, local copies, waits for them, and re-layouts: 0.34 us -> none  [network(): weights = jnp.pad(weights, ((0, 0), (0, 0), (0, 0), (0, 0), (0, 1), (0, 0)))]
where the time goes in v3:
time: 34.2 us; the launch traced here: 33.7 us
  Pallas kernels  21.6 us (63%)
  local copies, waits for them, and re-layouts  12 us (35%)
    pallas_call x1, Pallas kernels, rendered_window(): pl.pallas_call(render, out_shape=[jax.ShapeDtypeStruct(((YB + 2 * HALO) *...  14.4 us
    unnamed x32, local copies, waits for them, and re-layouts  12 us
    pallas_call x1, Pallas kernels, network(): pl.pallas_call(convolutions, out_shape=jax.ShapeDtypeStruct((channels, Z,...  7.25 us

profile of v3, /device:TPU:0, one launch (start us, length us, event | category | flops | bytes accessed | tf_op | source)
XLA Modules:
  0.0 33.7 jit_solution(8485445191749598746)
XLA Ops:
  0.0 0.0 copy-start
  0.0 0.9 %copy-done = bf16[8,128,128]{2,1,0:T(8,128)(2,1)S(1)} copy-done((bf16[8,128,128]{2,1,0:T(8,128)(2,1)S(1)}, bf16[8,128,128]{2,1,0:T(8,128)(2,1)}, u32[]{:S(2)}) %copy-start) | copy-done | bytes 262168
  1.0 0.0 copy-start.1
  1.0 0.9 %copy-done.1 = bf16[32,32,3,3,3]{1,0,4,3,2:T(8,128)(2,1)S(1)} copy-done((bf16[32,32,3,3,3]{1,0,4,3,2:T(8,128)(2,1)S(1)}, bf16[32,32,3,3,3]{1,0,4,3,2:T(8,128)(2,1)}, u32[]{:S(2)}) %copy-start.1) | copy-done | bytes 55320
  1.9 0.0 copy-start.2
  1.9 0.9 %copy-done.2 = bf16[32,32,3,3,3]{1,0,4,3,2:T(8,128)(2,1)S(1)} copy-done((bf16[32,32,3,3,3]{1,0,4,3,2:T(8,128)(2,1)S(1)}, bf16[32,32,3,3,3]{1,0,4,3,2:T(8,128)(2,1)}, u32[]{:S(2)}) %copy-start.2) | copy-done | bytes 55320
  2.8 0.0 copy-start.3
  2.8 0.9 %copy-done.3 = bf16[32,16,128]{2,1,0:T(8,128)(2,1)S(1)} copy-done((bf16[32,16,128]{2,1,0:T(8,128)(2,1)S(1)}, bf16[32,16,128]{2,1,0:T(8,128)(2,1)}, u32[]{:S(2)}) %copy-start.3) | copy-done | bytes 131096
  3.7 0.0 copy-start.4
  3.7 0.8 %copy-done.4 = bf16[27,1024]{1,0:T(8,128)(2,1)S(1)} copy-done((bf16[27,1024]{1,0:T(8,128)(2,1)S(1)}, bf16[27,1024]{1,0:T(8,128)(2,1)}, u32[]{:S(2)}) %copy-start.4) | copy-done | bytes 55320
  4.6 0.0 copy-start.5
  4.6 0.7 %copy-done.5 = bf16[8,8,16]{2,1,0:T(8,128)(2,1)S(1)} copy-done((bf16[8,8,16]{2,1,0:T(8,128)(2,1)S(1)}, bf16[8,8,16]{2,1,0:T(8,128)(2,1)}, u32[]{:S(2)}) %copy-start.5) | copy-done | bytes 2072
  5.3 0.0 copy-start.6
  5.3 0.7 %copy-done.6 = bf16[32,1,3,3,3]{0,4,3,2,1:T(4,128)(2,1)S(1)} copy-done((bf16[32,1,3,3,3]{0,4,3,2,1:T(4,128)(2,1)S(1)}, bf16[32,1,3,3,3]{0,4,3,2,1:T(4,128)(2,1)}, u32[]{:S(2)}) %copy-start.6) | copy-done | bytes 1752
  6.0 0.0 copy-start.7
  6.0 0.7 %copy-done.7 = s32[512,1]{0,1:T(1,128)S(1)} copy-done((s32[512,1]{0,1:T(1,128)S(1)}, s32[512,1]{0,1:T(1,128)}, u32[]{:S(2)}) %copy-start.7) | copy-done | bytes 2072
  6.7 0.0 copy-start.8
  6.7 0.7 %copy-done.8 = s32[512]{0:T(512)S(1)} copy-done((s32[512]{0:T(512)S(1)}, s32[512]{0:T(512)}, u32[]{:S(2)}) %copy-start.8) | copy-done | bytes 2072
  7.4 0.0 copy-start.9
  7.4 0.7 %copy-done.9 = s32[512]{0:T(512)S(1)} copy-done((s32[512]{0:T(512)S(1)}, s32[512]{0:T(512)}, u32[]{:S(2)}) %copy-start.9) | copy-done | bytes 2072
  8.0 0.0 copy-start.10
  8.0 0.7 %copy-done.10 = s32[512]{0:T(512)S(1)} copy-done((s32[512]{0:T(512)S(1)}, s32[512]{0:T(512)}, u32[]{:S(2)}) %copy-start.10) | copy-done | bytes 2072
  8.7 0.0 copy-start.11
  8.7 0.7 %copy-done.11 = s32[512]{0:T(512)S(1)} copy-done((s32[512]{0:T(512)S(1)}, s32[512]{0:T(512)}, u32[]{:S(2)}) %copy-start.11) | copy-done | bytes 2072
  9.4 0.0 copy-start.12
  9.4 0.7 %copy-done.12 = s32[512]{0:T(512)S(1)} copy-done((s32[512]{0:T(512)S(1)}, s32[512]{0:T(512)}, u32[]{:S(2)}) %copy-start.12) | copy-done | bytes 2072
  10.1 0.0 copy-start.13
  10.1 0.7 %copy-done.13 = f32[32]{0:T(128)S(1)} copy-done((f32[32]{0:T(128)S(1)}, f32[32]{0:T(128)}, u32[]{:S(2)}) %copy-start.13) | copy-done | bytes 152
  10.7 0.0 copy-start.14
  10.7 0.7 %copy-done.14 = f32[32]{0:T(128)S(1)} copy-done((f32[32]{0:T(128)S(1)}, f32[32]{0:T(128)}, u32[]{:S(2)}) %copy-start.14) | copy-done | bytes 152
  11.4 0.0 copy-start.15
  11.4 0.7 %copy-done.15 = f32[32]{0:T(128)S(1)} copy-done((f32[32]{0:T(128)S(1)}, f32[32]{0:T(128)}, u32[]{:S(2)}) %copy-start.15) | copy-done | bytes 152
  12.0 14.4 %render.1 = (bf16[56,512]{1,0:T(8,128)(2,1)S(1)}, bf16[256,128]{1,0:T(8,128)(2,1)S(1)}, bf16[2,256,1536]{2,1,0:T(8,128)(2,1)S(1)}, f32[256,128]{1,0:T(8,128)S(1)}) custom-call(bf16[512,128]{1,0:T(8,128)(2,1)S(1)} %bitcast.24, s32[4,128]{1,0:T(4,128)S(1)} %bitcast.27, s32[4,128]{1,0:T(4,128)S(1)} %bitcast.28, s32[4,128]{1,0:T(4,128)S(1)} %bitcast.29, ...), custom_call_target="tpu_custom_call" | custom-call | tf_op jit(solution)/shard_map/render/pallas_call | solution.py:282
  26.4 7.2 %network.1 = bf16[32,4,8,512]{3,2,1,0:T(8,128)(2,1)} custom-call(bf16[56,512]{1,0:T(8,128)(2,1)S(1)} %get-tuple-element.9.image_ref, bf16[256,128]{1,0:T(8,128)(2,1)S(1)} %get-tuple-element.10.taps_ref, bf16[2,256,1536]{2,1,0:T(8,128)(2,1)S(1)} %get-tuple-element.11.band, f32[256,128]{1,0:T(8,128)S(1)} %get-tuple-element.12.bias_ref), custom_call_target="tpu_custom_call" | custom-call | tf_op jit(solution)/shard_map/network/pallas_call | solution.py:401
Async XLA Ops:
  0.0 0.9 %copy-start = (bf16[8,128,128]{2,1,0:T(8,128)(2,1)S(1)}, bf16[8,128,128]{2,1,0:T(8,128)(2,1)}, u32[]{:S(2)}) copy-start(bf16[8,128,128]{2,1,0:T(8,128)(2,1)} %param.24) | copy-start | bytes 786436
  1.0 0.9 %copy-start.1 = (bf16[32,32,3,3,3]{1,0,4,3,2:T(8,128)(2,1)S(1)}, bf16[32,32,3,3,3]{1,0,4,3,2:T(8,128)(2,1)}, u32[]{:S(2)}) copy-start(bf16[32,32,3,3,3]{1,0,4,3,2:T(8,128)(2,1)} %param.27) | copy-start | bytes 165892
  1.9 0.9 %copy-start.2 = (bf16[32,32,3,3,3]{1,0,4,3,2:T(8,128)(2,1)S(1)}, bf16[32,32,3,3,3]{1,0,4,3,2:T(8,128)(2,1)}, u32[]{:S(2)}) copy-start(bf16[32,32,3,3,3]{1,0,4,3,2:T(8,128)(2,1)} %param.29) | copy-start | bytes 165892
  2.8 0.9 %copy-start.3 = (bf16[32,16,128]{2,1,0:T(8,128)(2,1)S(1)}, bf16[32,16,128]{2,1,0:T(8,128)(2,1)}, u32[]{:S(2)}) copy-start(bf16[32,16,128]{2,1,0:T(8,128)(2,1)} %param.16) | copy-start | bytes 393220
  3.7 0.8 %copy-start.4 = (bf16[27,1024]{1,0:T(8,128)(2,1)S(1)}, bf16[27,1024]{1,0:T(8,128)(2,1)}, u32[]{:S(2)}) copy-start(bf16[27,1024]{1,0:T(8,128)(2,1)} %constant.2.clone.spots_ref) | copy-start | bytes 165892
  4.6 0.7 %copy-start.5 = (bf16[8,8,16]{2,1,0:T(8,128)(2,1)S(1)}, bf16[8,8,16]{2,1,0:T(8,128)(2,1)}, u32[]{:S(2)}) copy-start(bf16[8,8,16]{2,1,0:T(8,128)(2,1)} %param.23) | copy-start | bytes 6148
  5.3 0.7 %copy-start.6 = (bf16[32,1,3,3,3]{0,4,3,2,1:T(4,128)(2,1)S(1)}, bf16[32,1,3,3,3]{0,4,3,2,1:T(4,128)(2,1)}, u32[]{:S(2)}) copy-start(bf16[32,1,3,3,3]{0,4,3,2,1:T(4,128)(2,1)} %param.25) | copy-start | bytes 5188
  6.0 0.7 %copy-start.7 = (s32[512,1]{0,1:T(1,128)S(1)}, s32[512,1]{0,1:T(1,128)}, u32[]{:S(2)}) copy-start(s32[512,1]{0,1:T(1,128)} %param.17) | copy-start | bytes 6148
  6.7 0.7 %copy-start.8 = (s32[512]{0:T(512)S(1)}, s32[512]{0:T(512)}, u32[]{:S(2)}) copy-start(s32[512]{0:T(512)} %param.18) | copy-start | bytes 6148
  7.4 0.7 %copy-start.9 = (s32[512]{0:T(512)S(1)}, s32[512]{0:T(512)}, u32[]{:S(2)}) copy-start(s32[512]{0:T(512)} %param.19) | copy-start | bytes 6148
  8.0 0.7 %copy-start.10 = (s32[512]{0:T(512)S(1)}, s32[512]{0:T(512)}, u32[]{:S(2)}) copy-start(s32[512]{0:T(512)} %param.20) | copy-start | bytes 6148
  8.7 0.7 %copy-start.11 = (s32[512]{0:T(512)S(1)}, s32[512]{0:T(512)}, u32[]{:S(2)}) copy-start(s32[512]{0:T(512)} %param.21) | copy-start | bytes 6148
  9.4 0.7 %copy-start.12 = (s32[512]{0:T(512)S(1)}, s32[512]{0:T(512)}, u32[]{:S(2)}) copy-start(s32[512]{0:T(512)} %param.22) | copy-start | bytes 6148
  10.1 0.7 %copy-start.13 = (f32[32]{0:T(128)S(1)}, f32[32]{0:T(128)}, u32[]{:S(2)}) copy-start(f32[32]{0:T(128)} %param.26) | copy-start | bytes 388
  10.7 0.7 %copy-start.14 = (f32[32]{0:T(128)S(1)}, f32[32]{0:T(128)}, u32[]{:S(2)}) copy-start(f32[32]{0:T(128)} %param.28) | copy-start | bytes 388
  11.4 0.7 %copy-start.15 = (f32[32]{0:T(128)S(1)}, f32[32]{0:T(128)}, u32[]{:S(2)}) copy-start(f32[32]{0:T(128)} %param.30) | copy-start | bytes 388

commit v4 on v3

--- a/solution.py
+++ b/solution.py
@@ -11,6 +11,7 @@
 Z = 4
 CAP = 4
 HALO = 3
+VMEM_BYTES = 67043328
 
 
 MESH = pl.DeviceIdType.MESH
@@ -67,7 +68,7 @@
         source = jnp.concatenate(
             [
                 jnp.concatenate(
-                    [deep[layer, (a * 3 + b) * 3 + c].astype(jnp.float32) for a in range(3)]
+                    [deep[layer][(a * 3 + b) * 3 + c].astype(jnp.float32) for a in range(3)]
                     + [jnp.zeros(square, jnp.float32)],
                     axis=1,
                 )
@@ -93,12 +94,21 @@
                         band[layer, rows : rows + channels, cols : cols + plane] = block
 
 
-def render(
-    tiles_ref, dest_ref, tile_ref, z_ref, xb_ref, ky_ref, kx_ref, wy_ref, wx_hbm,
-    spots_ref, w_first_ref, w_second_hbm, w_third_hbm, b_first_ref, b_second_ref, b_third_ref,
-    image_ref, taps_ref, band, bias_ref,
-    fields, sent, arrived, wx_ref, deep, send_sem, recv_sem, load_sem,
-):
+def render(*refs):
+    inputs = refs[:16]
+    image_ref = refs[16]
+    stored = refs[17:20]
+    held_inputs = refs[20:36]
+    taps_ref, band, bias_ref, fields, sent, arrived, send_sem, recv_sem, load_sem = refs[36:]
+    loads = [
+        pltpu.make_async_copy(source, target, load_sem.at[number])
+        for number, (source, target) in enumerate(zip(inputs, held_inputs))
+    ]
+    for load in loads:
+        load.start()
+    dest_ref, tile_ref, z_ref, xb_ref, ky_ref, kx_ref, wy_ref, tiles_ref = held_inputs[:8]
+    wx_ref, spots_ref, w_first_ref, w_second_ref, w_third_ref = held_inputs[8:13]
+    b_first_ref, b_second_ref, b_third_ref = held_inputs[13:]
     count = lax.axis_size("gy")
     own_index = lax.axis_index("gy")
     lines = sent.shape[1]
@@ -108,13 +118,6 @@
     window = YB + 2 * HALO
     order = sorted(range(1, count), key=lambda i: -min(i, count - i))
 
-    loads = [
-        pltpu.make_async_copy(w_second_hbm, deep.at[0], load_sem.at[0]),
-        pltpu.make_async_copy(w_third_hbm, deep.at[1], load_sem.at[1]),
-        pltpu.make_async_copy(wx_hbm, wx_ref, load_sem.at[2]),
-    ]
-    for load in loads:
-        load.start()
     arrived[:, live - live % 16 :, :] = jnp.zeros(
         (count, lines - live + live % 16, arrived.shape[2]), jnp.bfloat16
     )
@@ -124,6 +127,8 @@
             barrier, inc=1, device_id={"gy": lax.rem(own_index + i, count)}, device_id_type=MESH
         )
 
+    for load in loads[:6]:
+        load.wait()
     dest = dest_ref[...]
     place = iota(dest.shape, 1) % per_device
     rank = jnp.zeros_like(dest)
@@ -147,6 +152,8 @@
                 [row[line : line + 1] for row in rows], axis=0
             )
 
+    for load in loads[6:8]:
+        load.wait()
     own_group = own_index // GROUP
     mine = fields[own_group].astype(jnp.bfloat16)
     samples = per_device * YB
@@ -235,9 +242,16 @@
         )
         placed = onehot(iota((targets, depth), 0).astype(jnp.float32) == code)
         meta.append((source[:, 3:4], placed))
-    for load in loads:
+    for load in loads[8:]:
         load.wait()
+    deep = (w_second_ref, w_third_ref)
     arrange(spots_ref, w_first_ref, deep, b_first_ref, b_second_ref, b_third_ref, taps_ref, band, bias_ref)
+    stores = [
+        pltpu.make_async_copy(source, target, load_sem.at[len(inputs) + number])
+        for number, (source, target) in enumerate(zip((taps_ref, band, bias_ref), stored))
+    ]
+    for store in stores:
+        store.start()
     for copy in copies:
         copy.wait()
     for group in range(count // GROUP):
@@ -267,6 +281,8 @@
         image_ref[:, block * columns : (block + 1) * columns] = total[
             block * window * Z : (block + 1) * window * Z
         ].astype(jnp.bfloat16)
+    for store in stores:
+        store.wait()
 
 
 def rendered_window(tiles, entries, wy_table, wx_table, weights, biases):
@@ -276,9 +292,19 @@
     per_device = entries[0].size // count
     entries = [entry.reshape(-1, 128) for entry in entries]
     vmem = pl.BlockSpec(memory_space=pltpu.VMEM)
-    hbm = pl.BlockSpec(memory_space=pl.ANY)
+    hbm = pl.BlockSpec(memory_space=pltpu.HBM)
     channels = biases[0].shape[0]
     plane = Z * channels
+    inputs = [
+        *entries,
+        wy_table.reshape(-1, tile_rows),
+        tiles.reshape(tiles_dev * tile_rows, tile_cols),
+        wx_table.reshape(-1, tile_cols),
+        jnp.asarray(first_taps(), jnp.bfloat16),
+        weights[0].transpose(1, 2, 3, 4, 0).reshape(9, 3, channels),
+        *[weight.transpose(2, 3, 4, 0, 1).reshape(27, channels, channels) for weight in weights[1:]],
+        *[bias.reshape(1, channels) for bias in biases],
+    ]
     return pl.pallas_call(
         render,
         out_shape=[
@@ -287,32 +313,25 @@
             jax.ShapeDtypeStruct((2, 2 * plane, 12 * plane), jnp.bfloat16),
             jax.ShapeDtypeStruct((2 * plane, 128), jnp.float32),
         ],
-        in_specs=[vmem] * 8 + [hbm] + [vmem] * 2 + [hbm] * 2 + [vmem] * 3,
-        out_specs=[vmem] * 4,
-        scratch_shapes=[
+        in_specs=[hbm] * len(inputs),
+        out_specs=[vmem] + [hbm] * 3,
+        scratch_shapes=[pltpu.VMEM(value.shape, value.dtype) for value in inputs]
+        + [
+            pltpu.VMEM((2 * plane, 128), jnp.bfloat16),
+            pltpu.VMEM((2, 2 * plane, 12 * plane), jnp.bfloat16),
+            pltpu.VMEM((2 * plane, 128), jnp.float32),
             pltpu.VMEM((count // GROUP, 8, GROUP * per_device), jnp.float32),
             pltpu.VMEM((count, lines, tile_cols), jnp.bfloat16),
             pltpu.VMEM((count, lines, tile_cols), jnp.bfloat16),
-            pltpu.VMEM((wx_table.shape[0] * wx_table.shape[1], tile_cols), jnp.bfloat16),
-            pltpu.VMEM((2, 27, channels, channels), jnp.bfloat16),
             pltpu.SemaphoreType.DMA((count,)),
             pltpu.SemaphoreType.DMA((count,)),
-            pltpu.SemaphoreType.DMA((3,)),
+            pltpu.SemaphoreType.DMA((len(inputs) + 3,)),
         ],
         compiler_params=pltpu.CompilerParams(
-            collective_id=0, has_side_effects=True, vmem_limit_bytes=48 << 20
+            collective_id=0, has_side_effects=True, vmem_limit_bytes=VMEM_BYTES
         ),
         name="render",
-    )(
-        tiles.reshape(tiles_dev * tile_rows, tile_cols),
-        *entries,
-        wy_table.reshape(-1, tile_rows),
-        wx_table.reshape(-1, tile_cols),
-        first_taps().astype(jnp.bfloat16),
-        weights[0].transpose(1, 2, 3, 4, 0).reshape(9, 3, channels),
-        *[weight.transpose(2, 3, 4, 0, 1).reshape(27, channels, channels) for weight in weights[1:]],
-        *[bias.reshape(1, channels) for bias in biases],
-    )
+    )(*inputs)
 
 
 def first_taps():
@@ -337,7 +356,25 @@
     return before, value, after
 
 
-def convolutions(image_ref, taps_ref, band, bias_ref, out_ref, first, second, third):
+def convolutions(
+    image_hbm, taps_hbm, band_hbm, bias_hbm, out_ref,
+    image_ref, taps_ref, band, bias_ref, first, second, third, load_sem,
+):
+    loads = [
+        pltpu.make_async_copy(source, target, load_sem.at[number])
+        for number, (source, target) in enumerate(
+            (
+                (image_hbm, image_ref),
+                (taps_hbm, taps_ref),
+                (bias_hbm, bias_ref),
+                (band_hbm, band),
+            )
+        )
+    ]
+    for load in loads:
+        load.start()
+    for load in loads[:3]:
+        load.wait()
     own_index = lax.axis_index("gy")
     last_index = lax.axis_size("gy") - 1
     channels = out_ref.shape[0]
@@ -368,49 +405,49 @@
         result = jnp.dot(taps_ref[:, : 12 * Z], window, preferred_element_type=jnp.float32)
         keep(result + bias_ref[:, 0:1], first, pair, pairs, 2)
     depth = 12 * plane
+    loads[3].wait()
     for pair in range(YB // 2 + 1):
         window = first[6 * pair * plane : 6 * pair * plane + depth, :]
         result = jnp.dot(band[0], window, preferred_element_type=jnp.float32)
         keep(result + bias_ref[:, 1:2], second, pair, YB // 2 + 1, 1)
-    half = min(256, third.shape[0] * 128)
-    for start_x in range(0, third.shape[0] * 128, half):
-        blocks = range(start_x // 128, (start_x + half) // 128)
-        for pair in range(YB // 2):
-            rows = 6 * pair * plane
-            window = second[rows : rows + depth, start_x : start_x + half]
-            result = jnp.dot(band[1], window, preferred_element_type=jnp.float32)
-            result = jnp.maximum(result + bias_ref[:, 2:3], 0.0)
-            for yo in range(2):
-                for zo in range(Z):
-                    rows = (yo * Z + zo) * channels
-                    start = zo * YB + 2 * pair + yo
-                    for part, block in enumerate(blocks):
-                        third[block, pl.ds(start, channels, stride=Z * YB), :] = result[
-                            rows : rows + channels, part * 128 : (part + 1) * 128
-                        ]
-        for block in blocks:
-            out_ref[:, :, :, block * 128 : (block + 1) * 128] = (
-                third[block].reshape(channels, Z, YB, 128).astype(jnp.bfloat16)
-            )
+    for pair in range(YB // 2):
+        window = second[6 * pair * plane : 6 * pair * plane + depth, :]
+        result = jnp.dot(band[1], window, preferred_element_type=jnp.float32)
+        result = jnp.maximum(result + bias_ref[:, 2:3], 0.0).astype(jnp.bfloat16)
+        for yo in range(2):
+            for zo in range(Z):
+                rows = (yo * Z + zo) * channels
+                start = (2 * pair + yo) * channels
+                third[zo, start : start + channels, :] = result[rows : rows + channels]
+    size = YB * channels
+    line = iota((size, size), 0)
+    swap = onehot(iota((size, size), 1) == line % YB * channels + line // YB)
+    for zo in range(Z):
+        moved = jnp.dot(swap, third[zo], preferred_element_type=jnp.float32)
+        out_ref[:, zo, :, :] = moved.reshape(channels, YB, third.shape[2]).astype(jnp.bfloat16)
 
 
 def network(image, taps, band, biases, channels):
     width = image.shape[1]
     plane = Z * channels
     vmem = pl.BlockSpec(memory_space=pltpu.VMEM)
+    hbm = pl.BlockSpec(memory_space=pltpu.HBM)
+    inputs = (image, taps, band, biases)
     return pl.pallas_call(
         convolutions,
         out_shape=jax.ShapeDtypeStruct((channels, Z, YB, width), jnp.bfloat16),
-        in_specs=[vmem] * 4,
+        in_specs=[hbm] * 4,
         out_specs=vmem,
-        scratch_shapes=[
+        scratch_shapes=[pltpu.VMEM(value.shape, value.dtype) for value in inputs]
+        + [
             pltpu.VMEM((3 * plane * (YB + 4), width), jnp.bfloat16),
             pltpu.VMEM((3 * plane * (YB + 2), width), jnp.bfloat16),
-            pltpu.VMEM((width // 128, plane * YB, 128), jnp.float32),
+            pltpu.VMEM((Z, YB * channels, width), jnp.bfloat16),
+            pltpu.SemaphoreType.DMA((4,)),
         ],
-        compiler_params=pltpu.CompilerParams(vmem_limit_bytes=48 << 20),
+        compiler_params=pltpu.CompilerParams(vmem_limit_bytes=VMEM_BYTES),
         name="network",
-    )(image, taps, band, biases)
+    )(*inputs)
 
 
 def on_device(

time: 34.2 us -> 23.1 us (0.68); the launches traced: 33.7 us -> 22.9 us
  local copies, waits for them, and re-layouts: 12 us -> 0 us
  Pallas kernels: 21.6 us -> 22.9 us
    unnamed x32 -> x0, local copies, waits for them, and re-layouts: 12 us -> none
    pallas_call x1, Pallas kernels: 14.4 us -> 15.1 us  [rendered_window(): pl.pallas_call(render, out_shape=[jax.ShapeDtypeStruct(((YB + 2 * HALO) *...]
    pallas_call x1, Pallas kernels: 7.25 us -> 7.86 us  [network(): pl.pallas_call(convolutions, out_shape=jax.ShapeDtypeStruct((channels, Z,...]
where the time goes in v4:
time: 23.1 us; the launch traced here: 22.9 us
  Pallas kernels  22.9 us (99%)
    pallas_call x1, Pallas kernels, rendered_window(): pl.pallas_call(render, out_shape=[jax.ShapeDtypeStruct(((YB + 2 * HALO) *...  15.1 us
    pallas_call x1, Pallas kernels, network(): pl.pallas_call(convolutions, out_shape=jax.ShapeDtypeStruct((channels, Z,...  7.86 us

profile of v4, /device:TPU:0, one launch (start us, length us, event | category | flops | bytes accessed | tf_op | source)
XLA Modules:
  0.0 22.9 jit_solution(17647865306650386720)
XLA Ops:
  0.0 15.1 %render.1 = (bf16[56,512]{1,0:T(8,128)(2,1)}, bf16[256,128]{1,0:T(8,128)(2,1)}, bf16[2,256,1536]{2,1,0:T(8,128)(2,1)}, f32[256,128]{1,0:T(8,128)}) custom-call(s32[4,128]{1,0:T(4,128)} %bitcast.27, s32[4,128]{1,0:T(4,128)} %bitcast.28, s32[4,128]{1,0:T(4,128)} %bitcast.29, s32[4,128]{1,0:T(4,128)} %bitcast.30, s32[4,128]{1,0:T(4,128)} %bitcast.31, ...), custom_call_target="tpu_custom_call" | custom-call | tf_op jit(solution)/shard_map/render/pallas_call | solution.py:308
  15.1 7.9 %network.1 = bf16[32,4,8,512]{3,2,1,0:T(8,128)(2,1)} custom-call(bf16[56,512]{1,0:T(8,128)(2,1)} %get-tuple-element.9.image_hbm, bf16[256,128]{1,0:T(8,128)(2,1)} %get-tuple-element.10.taps_hbm, bf16[2,256,1536]{2,1,0:T(8,128)(2,1)} %get-tuple-element.11.band_hbm, f32[256,128]{1,0:T(8,128)} %get-tuple-element.12.bias_hbm), custom_call_target="tpu_custom_call" | custom-call | tf_op jit(solution)/shard_map/network/pallas_call | solution.py:436
